TPU v7x, 512 devices: a whole 4x4x16 slice. The times are simulated.
512 devices in a mesh: mode: 16 (over x, y), patch: 32 (over z, core).
Axes of the slice: x: 4, y: 4, z: 16, core: 2. Of those that a mesh axis runs over, the one named last changes fastest.
Arguments:
- flow_speed: bfloat16 [3, 2, 1024, 32768], P(None, None, 'mode', 'patch'), may hold values from -6 to 6
- heat_state: float32 [2, 1024, 32768], P(None, 'mode', 'patch'), may hold values from -6 to 6
- planar_slope_matrices: bfloat16 [128, 2, 256, 256], P('patch'), may hold values from -0.25 to 0.25
- conduction_matrices: bfloat16 [128, 256, 256], P('patch'), as said below
- adjacent_partners: int32 [128, 4], P('patch'), may hold values from 0 to 20, as said below
- opposite_direction_flags: int32 [128, 4], P('patch'), may hold values from 0 to 1
- interpatch_sides: int32 [32, 4], P('patch'), may hold values from 0 to 15, as said below
- liquid_cells: int32 [32], P('patch'), may hold values from 2 to 4, as said below
Outputs:
- new_temperature: float32 [2, 1024, 32768], P(None, 'mode', 'patch')
Inputs may be any that keep to these rules, and one draw needn't show every extreme that they name: `adjacent_partners`: element slots of a patch form a grid of 2 rows by 2 columns in an order drawn for each patch; partner faces are consistent both ways, walls across the chamber point at the zero trace. `interpatch_sides`: the first 2 entries name faces 0 of the first column, the rest faces 1 of the last column, by row. `liquid_cells`: some patch is fluid in all its elements. `conduction_matrices`: Symmetric; diagonal in 1 to 2, off-diagonal entries of magnitude at most 1 / sqrt(256).
All inputs are finite; a program needn't handle non-finite values.
Results may differ from a plain program's by a relative error of at most 0.0022.
Values may be sent and summed in bfloat16 or wider, within the bound.
A program may use at most 64 MiB of HBM per device.

v0:
```python
import math

import jax
import jax.numpy as jnp
from jax import lax
from jax.sharding import PartitionSpec as P

STEPS = 3


def with_halo(cells, sides, width):
    for axis, dim in sides:
        count = lax.axis_size(axis)
        head = lax.slice_in_dim(cells, 0, width, axis=dim)
        tail = lax.slice_in_dim(cells, cells.shape[dim] - width, cells.shape[dim], axis=dim)
        cells = jnp.concatenate(
            [
                lax.ppermute(tail, axis, [(i, (i + 1) % count) for i in range(count)]),
                cells,
                lax.ppermute(head, axis, [((i + 1) % count, i) for i in range(count)]),
            ],
            axis=dim,
        )
    return cells


def make_table(modes_all, points):
    index_m = jnp.arange(modes_all, dtype=jnp.int32)[:, None]
    index_z = jnp.arange(points, dtype=jnp.int32)[None, :]
    phase = index_m * index_z % points
    angle = phase.astype(jnp.float32) * jnp.float32(2.0 * math.pi / points)
    values = jnp.stack([jnp.cos(angle), -jnp.sin(angle)])
    return values.astype(jnp.bfloat16)


def apply_operator(v, stiff, adjacent_partners, opposite_direction_flags, interpatch_sides, factor):
    elems, edge, _, lanes = v.shape
    nodes = edge * edge
    rows = interpatch_sides.shape[1] // 2
    local = jnp.einsum(
        "eol,eno->enl", v.reshape(elems, nodes, lanes), stiff, precision=lax.Precision.HIGHEST
    ).reshape(elems, edge, edge, lanes)
    own = jnp.stack([v[:, 0], v[:, edge - 1], v[:, :, 0], v[:, :, edge - 1]], axis=1)
    own = own.reshape(elems * 4, edge, lanes)
    bound = own[interpatch_sides[0]]
    widened = with_halo(bound.astype(jnp.bfloat16), (("patch", 0),), rows).astype(bound.dtype)
    left = widened[:rows]
    right = widened[widened.shape[0] - rows :]
    zero = jnp.zeros((1, edge, lanes), jnp.float32)
    pool = jnp.concatenate([own, left, right, zero], axis=0)
    partner = pool[adjacent_partners.reshape(-1)]
    flipped = opposite_direction_flags.reshape(-1)[:, None, None] == 1
    partner = jnp.where(flipped, partner[:, ::-1], partner)
    jumps = (0.5 * (own - partner)).reshape(elems, 4, edge, lanes)
    middle_rows = jnp.zeros((elems, edge - 2, edge, lanes), jnp.float32)
    middle_cols = jnp.zeros((elems, edge, edge - 2, lanes), jnp.float32)
    lifted = jnp.concatenate([jumps[:, 0][:, None], middle_rows, jumps[:, 1][:, None]], axis=1)
    lifted = lifted + jnp.concatenate(
        [jumps[:, 2][:, :, None], middle_cols, jumps[:, 3][:, :, None]], axis=2
    )
    return factor * v + local + lifted


def per_device(
    flow_speed,
    heat_state,
    planar_slope_matrices,
    conduction_matrices,
    adjacent_partners,
    opposite_direction_flags,
    interpatch_sides,
    liquid_cells,
):
    mode_parts = lax.axis_size("mode")
    mode_count = flow_speed.shape[2]
    ndev = flow_speed.shape[3]
    elems = conduction_matrices.shape[0]
    nodes = conduction_matrices.shape[1]
    edge = math.isqrt(nodes)
    modes_all = mode_count * mode_parts
    points = 3 * modes_all
    block = ndev // mode_parts
    scale = math.sqrt(2.0 / points)
    table = make_table(modes_all, points)
    live = liquid_cells[0]
    sampled_quantity = jnp.concatenate([flow_speed, heat_state.astype(jnp.bfloat16)[None]], axis=0)
    spread = lax.all_to_all(sampled_quantity, "mode", split_axis=3, concat_axis=2, tiled=True)
    phys = jnp.einsum("fcmb,cmz->fbz", spread, table, preferred_element_type=jnp.float32) * scale
    flux = phys[:3] * phys[3:4]
    start = lax.axis_index("mode") * block
    node_ids = start + jnp.arange(block, dtype=jnp.int32)
    wet = (node_ids // nodes < live).astype(jnp.float32)
    flux = flux * wet[None, :, None]
    flux = flux.astype(jnp.bfloat16)
    coeffs = jnp.einsum("fbz,cmz->fcmb", flux, table, preferred_element_type=jnp.float32) * scale
    flux_hat = lax.all_to_all(
        coeffs.astype(jnp.bfloat16), "mode", split_axis=2, concat_axis=3, tiled=True
    )
    lanes = 2 * mode_count
    first_mode = lax.axis_index("mode") * mode_count
    harmonic_index = (first_mode + jnp.arange(mode_count, dtype=jnp.int32)).astype(
        jnp.float32
    ) / modes_all
    sectional_slice = flux_hat[:2].reshape(2, 2, mode_count, elems, nodes)
    transport = jnp.einsum(
        "rsxfq,frhq->fhsx",
        sectional_slice,
        planar_slope_matrices,
        preferred_element_type=jnp.float32,
    ).reshape(elems, nodes, lanes)
    lengthwise = flux_hat[2].astype(jnp.float32)
    azimuthal = jnp.stack(
        [-harmonic_index[:, None] * lengthwise[1], harmonic_index[:, None] * lengthwise[0]]
    )
    azimuthal = jnp.transpose(azimuthal, (2, 0, 1)).reshape(elems, nodes, lanes)
    heat_nodes = jnp.transpose(heat_state, (2, 0, 1)).reshape(elems, nodes, lanes)
    forcing_vector = (heat_nodes - 0.5 * (transport + azimuthal)).reshape(elems, edge, edge, lanes)
    stiff = conduction_matrices.astype(jnp.float32)
    lane_index = jnp.concatenate([harmonic_index, harmonic_index])
    factor = (1.0 + lane_index * lane_index)[None, None, None, :]
    theta, delta = (4.0, 3.0)
    sigma = theta / delta
    solution = jnp.zeros_like(forcing_vector)
    resid = forcing_vector
    walk = resid / theta
    rho = 1.0 / sigma
    for step in range(STEPS):
        image = apply_operator(
            walk, stiff, adjacent_partners, opposite_direction_flags, interpatch_sides, factor
        )
        solution = solution + walk
        resid = resid - image
        rho_new = 1.0 / (2.0 * sigma - rho)
        walk = rho_new * rho * walk + 2.0 * rho_new / delta * resid
        rho = rho_new
    final = (solution + walk).reshape(ndev, 2, mode_count)
    return jnp.transpose(final, (1, 2, 0))


def solution(mesh):
    placed = (
        P(None, None, "mode", "patch"),
        P(None, "mode", "patch"),
        P("patch", None, None, None),
        P("patch", None, None),
        P("patch", None),
        P("patch", None),
        P("patch", None),
        P("patch"),
    )
    return jax.shard_map(
        per_device, mesh=mesh, in_specs=placed, out_specs=P(None, "mode", "patch"), check_vma=False
    )
```

profile of v0, /device:TPU:6, one launch (start us, length us, event | category | flops | bytes accessed | tf_op | source)
XLA Modules:
  0.0 223.7 jit_solution(1042815818747012435)
XLA Ops:
  2.5 2.6 %copy.105 = bf16[4,2,64,1024]{2,0,1,3:T(4,128)(2,1)} copy(bf16[4,2,64,1024]{3,2,1,0:T(8,128)(2,1)S(1)} %pad_maximum_fusion.3) | data formatting | bytes 2097152 | tf_op jit(solution)/shard_map/concatenate | solution.py:86
  5.1 5.1 %reshape.381 = bf16[16,2,16384]{2,1,0:T(2,128)(2,1)} reshape(bf16[1024,2,4,64]{3,2,1,0:T(4,128)(2,1)} %bitcast.163) | data formatting | bytes 2097152
  10.1 9.4 %all-to-all-start = ((bf16[16,2,16384]{2,1,0:T(2,128)(2,1)}), bf16[16,2,16384]{2,1,0:T(2,128)(2,1)S(1)}, u32[]{:S(2)}, u32[]{:S(2)}) async-start(bf16[16,2,16384]{2,1,0:T(2,128)(2,1)} %reshape.381), calls=%async_computation | async-start | bytes 2097152 | tf_op jit(solution)/shard_map/all_to_all | solution.py:87
  23.1 2.6 %reshape.306 = f32[4,16,16,128]{3,2,1,0:T(8,128)} reshape(f32[1024,2,64]{2,1,0:T(2,128)} %copy.114) | data formatting | bytes 1048576 | tf_op jit(solution)/shard_map/reshape | solution.py:116
  28.4 52.8 %negate_convert_fusion = (bf16[1,1024,3072]{2,1,0:T(8,128)(2,1)}, bf16[1,1024,3072]{2,1,0:T(8,128)(2,1)}) fusion(), kind=kLoop, calls=%fused_computation.14 | loop fusion | flops 37748736 | bytes 12582912 | tf_op jit(solution)/shard_map/convert.1
  81.2 2.3 %reshape.382 = bf16[1024,2,4,64]{3,2,1,0:T(4,128)(2,1)} reshape(bf16[16,2,16384]{2,1,0:T(2,128)(2,1)S(1)} %all-to-all-done) | data formatting | bytes 2097152
  83.5 4.2 %copy.162 = bf16[4,2,64,16,64]{2,3,4,1,0:T(8,128)(2,1)} copy(bf16[4,2,64,16,64]{2,0,1,4,3:T(4,128)(2,1)} %bitcast.164) | data formatting | bytes 2097152 | tf_op jit(solution)/shard_map/all_to_all | solution.py:87
  87.8 3.2 %all_to_all.27 = bf16[4,2,1024,64]{2,3,1,0:T(8,128)(2,1)S(1)} reshape(bf16[4,2,16,64,64]{3,2,4,1,0:T(8,128)(2,1)} %bitcast.165) | data formatting | bytes 2097152 | tf_op jit(solution)/shard_map/all_to_all | solution.py:87
  91.0 6.5 %fusion.12 = f32[4,64,3072]{2,1,0:T(8,128)S(1)} fusion(bf16[4,2,1024,64]{2,3,1,0:T(8,128)(2,1)S(1)} %all_to_all.27, bf16[1,1024,3072]{2,1,0:T(8,128)(2,1)} %get-tuple-element.51, bf16[1,1024,3072]{2,1,0:T(8,128)(2,1)} %get-tuple-element.52), kind=kOutput, calls=%fused_computation.21 | convolution fusion | flops 3228303360 | bytes 16777216 | tf_op jit(solution)/shard_map/fcmb,cmz->fbz/dot_general | solution.py:88
  97.6 8.6 %fusion.19 = bf16[3,2,1024,64]{2,3,0,1:T(8,128)(2,1)} fusion(bf16[1,1024,3072]{2,1,0:T(8,128)(2,1)} %get-tuple-element.51, bf16[1,1024,3072]{2,1,0:T(8,128)(2,1)} %get-tuple-element.52, f32[4,64,3072]{2,1,0:T(8,128)S(1)} %fusion.12, f32[64]{0:T(128)S(1)} %compare_convert_fusion, f32[64,3072]{1,0:T(8,128)S(1)} %slice_bitcast_fusion), kind=kOutput, calls=%fused_computation.28 | convolution fusion | flops 2443640832 | bytes 16515584 | tf_op jit(solution)/shard_map/fbz,cmz->fcmb/dot_general | solution.py:95
  106.2 4.2 %copy.107 = bf16[3,2,1024,64]{3,1,0,2:T(2,128)(2,1)S(1)} copy(bf16[3,2,1024,64]{2,3,0,1:T(8,128)(2,1)} %fusion.19) | data formatting | bytes 1572864 | tf_op jit(solution)/shard_map/convert_element_type | solution.py:97
  110.4 1.9 reshape.383
  112.3 7.2 %all-to-all-start.1 = ((bf16[16,2,12288]{2,1,0:T(2,128)(2,1)}), bf16[16,2,12288]{2,1,0:T(2,128)(2,1)}, u32[]{:S(2)}, u32[]{:S(2)}) async-start(bf16[16,2,12288]{2,1,0:T(2,128)(2,1)} %reshape.383), calls=%async_computation.1 | async-start | bytes 1572864 | tf_op jit(solution)/shard_map/all_to_all | solution.py:96
  121.5 7.9 %all-to-all-done.1 = bf16[16,2,12288]{2,1,0:T(2,128)(2,1)} async-done(((bf16[16,2,12288]{2,1,0:T(2,128)(2,1)}), bf16[16,2,12288]{2,1,0:T(2,128)(2,1)}, u32[]{:S(2)}, u32[]{:S(2)}) %all-to-all-start.1) | async-done | bytes 786464 | tf_op jit(solution)/shard_map/all_to_all | solution.py:96
  129.4 4.0 %reshape.384 = bf16[1024,3,2,64]{3,2,1,0:T(2,128)(2,1)S(1)} reshape(bf16[16,2,12288]{2,1,0:T(2,128)(2,1)} %all-to-all-done.1) | data formatting | bytes 1572864
  139.0 2.8 %reshape.300 = bf16[2,2,64,4,256]{4,3,2,1,0:T(4,128)(2,1)} reshape(bf16[2,2,64,16,64]{4,3,2,1,0:T(8,128)(2,1)} %slice.192) | data formatting | bytes 1048576 | tf_op jit(solution)/shard_map/reshape | solution.py:104
  144.6 2.6 %reshape.307 = f32[4,16,16,128]{3,2,1,0:T(8,128)} reshape(f32[4,256,2,64]{3,2,1,0:T(2,128)} %copy.115) | data formatting | bytes 1048576 | tf_op jit(solution)/shard_map/reshape | solution.py:110
  147.2 2.1 broadcast_multiply_fusion
  151.0 7.1 %collective-permute-start.1 = (bf16[2,16,128]{2,1,0:T(8,128)(2,1)}, bf16[2,16,128]{2,1,0:T(8,128)(2,1)}, u32[]{:S(2)}, u32[]{:S(2)}) collective-permute-start(bf16[2,16,128]{2,1,0:T(8,128)(2,1)} %get-tuple-element.50), channel_id=1, source_target_pairs={{1,0},{2,1},{3,2},{4,3},{5,4},{6,5},{7,6},{8,7},{9,8},{10,9},{11,1... | collective-permute-start | bytes 24584 | tf_op jit(solution)/shard_map/ppermute | solution.py:20
  163.1 2.1 reshape.305
  172.9 3.0 %collective-permute-start.3 = (bf16[2,16,128]{2,1,0:T(8,128)(2,1)}, bf16[2,16,128]{2,1,0:T(8,128)(2,1)}, u32[]{:S(2)}, u32[]{:S(2)}) collective-permute-start(bf16[2,16,128]{2,1,0:T(8,128)(2,1)} %get-tuple-element.48), channel_id=1, source_target_pairs={{1,0},{2,1},{3,2},{4,3},{5,4},{6,5},{7,6},{8,7},{9,8},{10,9},{11,1... | collective-permute-start | bytes 24584 | tf_op jit(solution)/shard_map/ppermute | solution.py:20
  179.9 2.6 %add.232 = f32[1024,2,64]{2,1,0:T(2,128)} reshape(f32[4,16,16,128]{3,2,1,0:T(8,128)} %copy-done.2) | data formatting | bytes 1048576 | tf_op jit(solution)/shard_map/add | solution.py:58
  182.5 2.1 reshape.312
  184.6 2.1 copy.122
  188.9 2.2 %gather_fusion.3 = f32[16,16,128]{2,1,0:T(8,128)} fusion(f32[21,16,128]{2,1,0:T(8,128)} %maximum_maximum_fusion.1, s32[1024]{0:T(1024)} %pad_clamp_fusion), kind=kCustom, calls=%fused_computation.3 | custom fusion | bytes 262208 | tf_op jit(solution)/shard_map/gather | solution.py:51
  193.8 2.7 %maximum_add_fusion.1 = (f32[4,16,16,128]{3,2,1,0:T(8,128)}, f32[4,16,16,128]{3,2,1,0:T(8,128)S(1)}) fusion(f32[4,1,16,128]{3,2,1,0:T(8,128)S(1)} %get-tuple-element.34, f32[4,1,16,128]{3,2,1,0:T(8,128)S(1)} %get-tuple-element.31, f32[4,16,1,128]{3,2,1,0:T(1,128)S(1)} %bitcast.191, f32[4,16,1,128]{3,2,1,0:T(1,128)S(1)} %bitcast.192, f32[16]{0:T(128)} %pad.40.clone, ...), kind=kLoop, calls=%fused_computation.42 | loop fusion | flops 3145728 | bytes 2884672 | tf_op jit(solution)/shard_map/add | solution.py:58
  196.5 2.0 copy.132
  199.8 3.0 %collective-permute-start.5 = (bf16[2,16,128]{2,1,0:T(8,128)(2,1)}, bf16[2,16,128]{2,1,0:T(8,128)(2,1)}, u32[]{:S(2)}, u32[]{:S(2)}) collective-permute-start(bf16[2,16,128]{2,1,0:T(8,128)(2,1)} %get-tuple-element.46), channel_id=1, source_target_pairs={{1,0},{2,1},{3,2},{4,3},{5,4},{6,5},{7,6},{8,7},{9,8},{10,9},{11,1... | collective-permute-start | bytes 24584 | tf_op jit(solution)/shard_map/ppermute | solution.py:20
  202.8 3.0 %convolution_bitcast_fusion = f32[4,256,128]{1,2,0:T(8,128)} fusion(bf16[4,256,256]{2,1,0:T(8,128)(2,1)} %param.11, f32[4,256,128]{1,2,0:T(8,128)} %copy.132, f32[4,256,128]{1,2,0:T(8,128)S(1)} %convolution_bitcast_fusion.1, f32[4,256,128]{1,2,0:T(8,128)S(1)} %fusion.29, f32[128]{0:T(128)} %get-tuple-element.6, f32[4,256,128]{1,2,0:T(8,128)} %copy.123, ...), kind=kOutput, calls=%fused_computation.29 | convolution fusion | flops 404488192 | bytes 3671040 | tf_op jit(solution)/shard_map/eol,eno->enl/dot_general | solution.py:40
  207.5 2.2 copy.133
  209.7 2.1 reshape.316
  220.3 3.4 %add_bitcast_fusion = f32[2,64,1024]{2,1,0:T(8,128)} fusion(f32[1024,2,64]{0,2,1:T(8,128)} %copy.140, f32[1024,2,64]{0,2,1:T(8,128)} %reshape.316, f32[1024,2,64]{0,2,1:T(8,128)} %copy.131, f32[1024,2,64]{0,2,1:T(8,128)} %reshape.312, f32[1024,2,64]{0,2,1:T(8,128)} %copy.122, f32[1024,2,64]{0,2,1:T(8,128)} %reshape.305, f32[1024,2,64]{0,2,1:T(8,128)} %bitcast.176, ...), kind=kLoop, calls=%fused_computation.48 | loop fusion | flops 3801088 | bytes 5243904 | tf_op jit(solution)/shard_map/transpose | solution.py:137
  (124 shorter events, 52.8 us)
Async XLA Ops:
  0.0 141.8 %copy-start = (bf16[4,2,256,256]{3,2,1,0:T(8,128)(2,1)S(1)}, bf16[4,2,256,256]{3,2,1,0:T(8,128)(2,1)}, u32[]{:S(2)}) copy-start(bf16[4,2,256,256]{3,2,1,0:T(8,128)(2,1)} %param.10) | copy-start | bytes 3145732
  0.0 20.8 %copy-start.1 = (f32[2,64,1024]{2,1,0:T(8,128)S(1)}, f32[2,64,1024]{2,1,0:T(8,128)}, u32[]{:S(2)}) copy-start(f32[2,64,1024]{2,1,0:T(8,128)} %param.9) | copy-start | bytes 1572868
  0.0 20.2 %copy-start.11 = (s32[4,4]{1,0:T(4,128)S(1)}, s32[4,4]{1,0:T(4,128)}, u32[]{:S(2)}) copy-start(s32[4,4]{1,0:T(4,128)} %param.13) | copy-start | bytes 196
  2.4 23.3 %copy-start.12 = (s32[4,4]{1,0:T(4,128)S(1)}, s32[4,4]{1,0:T(4,128)}, u32[]{:S(2)}) copy-start(s32[4,4]{1,0:T(4,128)} %param.12) | copy-start | bytes 196
  10.1 71.1 %all-to-all-start = ((bf16[16,2,16384]{2,1,0:T(2,128)(2,1)}), bf16[16,2,16384]{2,1,0:T(2,128)(2,1)S(1)}, u32[]{:S(2)}, u32[]{:S(2)}) async-start(bf16[16,2,16384]{2,1,0:T(2,128)(2,1)} %reshape.381), calls=%async_computation | async-start | bytes 2097152 | tf_op jit(solution)/shard_map/all_to_all | solution.py:87
  20.8 60.4 %copy-start.10 = (f32[128]{0:T(128)}, f32[128]{0:T(128)S(1)}, u32[]{:S(2)}) copy-start(f32[128]{0:T(128)S(1)} %get-tuple-element.5) | copy-start | bytes 1540
  106.2 14.0 %copy-start.13 = (s32[1,4]{1,0:T(1,128)S(1)}, s32[1,4]{1,0:T(1,128)}, u32[]{:S(2)}) copy-start(s32[1,4]{1,0:T(1,128)} %param.14) | copy-start | bytes 52
  112.3 17.1 %all-to-all-start.1 = ((bf16[16,2,12288]{2,1,0:T(2,128)(2,1)}), bf16[16,2,12288]{2,1,0:T(2,128)(2,1)}, u32[]{:S(2)}, u32[]{:S(2)}) async-start(bf16[16,2,12288]{2,1,0:T(2,128)(2,1)} %reshape.383), calls=%async_computation.1 | async-start | bytes 1572864 | tf_op jit(solution)/shard_map/all_to_all | solution.py:96
  136.3 0.7 copy-start.3
  139.0 8.2 %copy-start.5 = (f32[4,16,16,128]{3,2,1,0:T(8,128)S(1)}, f32[4,16,16,128]{3,2,1,0:T(8,128)}, u32[]{:S(2)}) copy-start(f32[4,16,16,128]{3,2,1,0:T(8,128)} %reshape.306) | copy-start | bytes 1572868
  151.0 15.1 %collective-permute-start = (bf16[2,16,128]{2,1,0:T(8,128)(2,1)}, bf16[2,16,128]{2,1,0:T(8,128)(2,1)}, u32[]{:S(2)}, u32[]{:S(2)}) collective-permute-start(bf16[2,16,128]{2,1,0:T(8,128)(2,1)} %get-tuple-element.49), channel_id=1, source_target_pairs={{0,1},{1,2},{2,3},{3,4},{4,5},{5,6},{6,7},{7,8},{8,9},{9,10},{10,1... | collective-permute-start | bytes 24584 | tf_op jit(solution)/shard_map/ppermute | solution.py:18
  151.0 15.1 %collective-permute-start.1 = (bf16[2,16,128]{2,1,0:T(8,128)(2,1)}, bf16[2,16,128]{2,1,0:T(8,128)(2,1)}, u32[]{:S(2)}, u32[]{:S(2)}) collective-permute-start(bf16[2,16,128]{2,1,0:T(8,128)(2,1)} %get-tuple-element.50), channel_id=1, source_target_pairs={{1,0},{2,1},{3,2},{4,3},{5,4},{6,5},{7,6},{8,7},{9,8},{10,9},{11,1... | collective-permute-start | bytes 24584 | tf_op jit(solution)/shard_map/ppermute | solution.py:20
  168.9 1.6 copy-start.6
  168.9 1.6 copy-start.7
  169.0 1.6 copy-start.8
  169.0 1.6 copy-start.9
  170.4 2.4 %copy-start.2 = (f32[4,16,16,128]{3,2,1,0:T(8,128)}, f32[4,16,16,128]{3,2,1,0:T(8,128)S(1)}, u32[]{:S(2)}) copy-start(f32[4,16,16,128]{3,2,1,0:T(8,128)S(1)} %get-tuple-element.26) | copy-start | bytes 1572868
  172.9 13.9 %collective-permute-start.2 = (bf16[2,16,128]{2,1,0:T(8,128)(2,1)}, bf16[2,16,128]{2,1,0:T(8,128)(2,1)}, u32[]{:S(2)}, u32[]{:S(2)}) collective-permute-start(bf16[2,16,128]{2,1,0:T(8,128)(2,1)} %get-tuple-element.47), channel_id=1, source_target_pairs={{0,1},{1,2},{2,3},{3,4},{4,5},{5,6},{6,7},{7,8},{8,9},{9,10},{10,1... | collective-permute-start | bytes 24584 | tf_op jit(solution)/shard_map/ppermute | solution.py:18
  172.9 13.9 %collective-permute-start.3 = (bf16[2,16,128]{2,1,0:T(8,128)(2,1)}, bf16[2,16,128]{2,1,0:T(8,128)(2,1)}, u32[]{:S(2)}, u32[]{:S(2)}) collective-permute-start(bf16[2,16,128]{2,1,0:T(8,128)(2,1)} %get-tuple-element.48), channel_id=1, source_target_pairs={{1,0},{2,1},{3,2},{4,3},{5,4},{6,5},{7,6},{8,7},{9,8},{10,9},{11,1... | collective-permute-start | bytes 24584 | tf_op jit(solution)/shard_map/ppermute | solution.py:20
  199.8 13.1 %collective-permute-start.4 = (bf16[2,16,128]{2,1,0:T(8,128)(2,1)}, bf16[2,16,128]{2,1,0:T(8,128)(2,1)}, u32[]{:S(2)}, u32[]{:S(2)}) collective-permute-start(bf16[2,16,128]{2,1,0:T(8,128)(2,1)} %get-tuple-element.45), channel_id=1, source_target_pairs={{0,1},{1,2},{2,3},{3,4},{4,5},{5,6},{6,7},{7,8},{8,9},{9,10},{10,1... | collective-permute-start | bytes 24584 | tf_op jit(solution)/shard_map/ppermute | solution.py:18
  199.8 13.1 %collective-permute-start.5 = (bf16[2,16,128]{2,1,0:T(8,128)(2,1)}, bf16[2,16,128]{2,1,0:T(8,128)(2,1)}, u32[]{:S(2)}, u32[]{:S(2)}) collective-permute-start(bf16[2,16,128]{2,1,0:T(8,128)(2,1)} %get-tuple-element.46), channel_id=1, source_target_pairs={{1,0},{2,1},{3,2},{4,3},{5,4},{6,5},{7,6},{8,7},{9,8},{10,9},{11,1... | collective-permute-start | bytes 24584 | tf_op jit(solution)/shard_map/ppermute | solution.py:20
  205.8 14.5 %copy-start.4 = (f32[1,64,1024]{2,1,0:T(8,128)S(1)}, f32[1,64,1024]{2,1,0:T(8,128)}, u32[]{:S(2)}) copy-start(f32[1,64,1024]{2,1,0:T(8,128)} %copy-done.3) | copy-start | bytes 786436
where the time goes:
time: 226 us; the launch traced here: 224 us
  local copies, waits for them, and re-layouts  84.4 us (37%)
  other arithmetic  77.4 us (34%)
  starting transfers between devices  29.6 us (13%)
  matrix products  23.2 us (10%)
  waiting for transfers between devices  7.95 us (4%)
    another operation x1, other arithmetic  52.8 us
    unnamed x35, local copies, waits for them, and re-layouts  14.1 us
    add x8, local copies, waits for them, and re-layouts, apply_operator(): lifted + jnp.concatenate([jumps[:, 2][:, :, None], middle_cols, jumps[:,...  13.5 us
    ppermute x3, starting transfers between devices, with_halo(): lax.ppermute(head, axis, [((i + 1) % count, i) for i in range(count)])  13 us
    all_to_all x1, starting transfers between devices, per_device(): lax.all_to_all(sampled_quantity, 'mode', split_axis=3, concat_axis=2, til...  9.37 us
    dot_general x1, matrix products, per_device(): jnp.einsum('fbz,cmz->fcmb', flux, table, preferred_element_type=jnp.float32)  8.65 us
    all_to_all x1, waiting for transfers between devices, per_device(): lax.all_to_all(coeffs.astype(jnp.bfloat16), 'mode', split_axis=2, concat_...  7.93 us
    all_to_all x2, local copies, waits for them, and re-layouts, per_device(): lax.all_to_all(sampled_quantity, 'mode', split_axis=3, concat_axis=2, til...  7.48 us
  transfers between devices with their start and end apart: 8, of which 1 were waited for; matrix products, arithmetic and copies ran while one was open for 41% of the time, Pallas kernels for 0%

commit v1 on v0

v1 whole, which is shorter than its diff:
```python
import functools
import math

import jax
import jax.numpy as jnp
import numpy as np
from jax import lax
from jax.experimental import pallas as pl
from jax.experimental.pallas import tpu as pltpu
from jax.sharding import PartitionSpec as P

STEPS = 3
MESH = pl.DeviceIdType.MESH
F32 = jnp.float32
BF16 = jnp.bfloat16


def tables(modes, points, rows):
    half = points // 2
    z = np.arange(half + 1)
    m = np.arange(modes)
    phase = (z[:, None] * m[None, :]) % points
    angle = phase.astype(np.float32) * np.float32(2.0 * math.pi / points)
    out = np.zeros((2, rows, modes), np.float32)
    out[0, : half + 1] = np.cos(angle)
    out[1, : half + 1] = -np.sin(angle)
    out = out.astype(BF16)
    back = np.swapaxes(out, 1, 2).astype(np.float32)
    back[:, :, 0] *= 0.5
    back[:, :, half] *= 0.5
    return out, np.ascontiguousarray(back).astype(BF16)


def lift_table(elems, edge):
    nodes = edge * edge
    out = np.zeros((elems * 4 * edge, elems * nodes), np.float32)
    for e in range(elems):
        for i in range(edge):
            for face, node in enumerate((i, (edge - 1) * edge + i, i * edge, i * edge + edge - 1)):
                out[(e * 4 + face) * edge + i, e * nodes + node] = 1.0
    return out


def dot(a, b):
    return jnp.dot(a, b, preferred_element_type=F32)


def dot_nt(a, b):
    return lax.dot_general(a, b, (((1,), (1,)), ((), ())), preferred_element_type=F32)


def kernel(
    sizes,
    partners_ref,
    flags_ref,
    sides_ref,
    live_ref,
    flow_hbm,
    heat_hbm,
    slope_hbm,
    stiff_hbm,
    out_table_hbm,
    back_table_hbm,
    lift_hbm,
    lift_t_hbm,
    result_ref,
    flow,
    heat,
    slope,
    stiff,
    out_table,
    back_table,
    lift,
    lift_t,
    send1,
    recv1,
    flux_c,
    flux_s,
    send2,
    recv2,
    weights,
    dense,
    pick,
    halo_lift,
    halves,
    traces,
    halo,
    load_sem,
    own_sem,
    send1_sem,
    recv1_sem,
    send2_sem,
    recv2_sem,
    halo_send_sem,
    halo_recv_sem,
):
    parts, patches, mode_count, ndev, elems, edge, points = sizes
    modes = mode_count * parts
    nodes = edge * edge
    half = points // 2
    me = lax.axis_index("mode")
    patch = lax.axis_index("patch")
    left = lax.rem(patch + patches - 1, patches)
    right = lax.rem(patch + 1, patches)
    scale = math.sqrt(2.0 / points)

    loads = [
        pltpu.make_async_copy(src, dst, load_sem.at[i])
        for i, (src, dst) in enumerate(
            (
                (heat_hbm, heat),
                (flow_hbm, flow),
                (out_table_hbm, out_table),
                (back_table_hbm, back_table),
                (slope_hbm, slope),
                (stiff_hbm, stiff),
                (lift_hbm, lift),
                (lift_t_hbm, lift_t),
            )
        )
    ]
    for load in loads:
        load.start()

    barrier = pltpu.get_barrier_semaphore()
    for k in range(1, parts):
        pl.semaphore_signal(
            barrier, inc=1, device_id=(lax.rem(me + k, parts), patch), device_id_type=MESH
        )
    for side in (left, right):
        pl.semaphore_signal(barrier, inc=1, device_id=(me, side), device_id_type=MESH)

    low = lax.broadcasted_iota(jnp.int32, (mode_count, 128), 1) < 64

    def split(a, b):
        mask = lax.broadcasted_iota(jnp.int32, a.shape, 1) < 64
        return (
            jnp.where(mask, a, pltpu.roll(b, 64, 1)),
            jnp.where(mask, pltpu.roll(a, 64, 1), b),
        )

    loads[0].wait()
    loads[1].wait()
    barred = False
    for step in range(parts // 2):
        tile = lax.rem(me // 2 + step, parts // 2)
        cols = pl.ds(pl.multiple_of(tile * 128, 128), 128)
        for c in range(2):
            fields = [flow[f, c, :, cols].astype(F32) for f in range(3)]
            fields.append(heat[c, :, cols].astype(BF16).astype(F32))
            for pair in range(2):
                even, odd = split(fields[2 * pair], fields[2 * pair + 1])
                lanes = slice(128 * pair, 128 * pair + 128)
                send1[2 * tile, c, :, lanes] = even.astype(BF16)
                send1[2 * tile + 1, c, :, lanes] = odd.astype(BF16)
        if not barred:
            pl.semaphore_wait(barrier, parts + 1)
            barred = True
            own = pltpu.make_async_copy(
                send1.at[me], recv1.at[:, pl.ds(me * mode_count, mode_count), :], own_sem
            )
            own.start()
            other = lax.rem(me, 2)
            dests = [2 * tile + 1 - other]
        else:
            dests = [2 * tile, 2 * tile + 1]
        for dest in dests:
            pltpu.make_async_remote_copy(
                send1.at[dest],
                recv1.at[:, pl.ds(me * mode_count, mode_count), :],
                send1_sem.at[dest],
                recv1_sem.at[me],
                device_id=(dest, patch),
                device_id_type=MESH,
            ).start()

    for load in loads[2:]:
        load.wait()
    lane = lax.broadcasted_iota(jnp.int32, (1, 256), 1)
    group, offset = lane // edge, lane % edge
    source = jnp.full((1, 256), -1, jnp.int32)
    for e in range(elems):
        for face in range(4):
            there = jnp.where(flags_ref[e, face] == 1, edge - 1 - offset, offset)
            source = jnp.where(
                group == e * 4 + face, partners_ref[e, face] * edge + there, source
            )
    row = lax.broadcasted_iota(jnp.int32, (256, 256), 0)
    inner = jnp.where(row == source, 1.0, 0.0).astype(BF16)
    inner = dot(inner, lift[...]).astype(BF16)
    row = lax.broadcasted_iota(jnp.int32, (128, 256), 0)
    wanted = jnp.where(row < 2 * edge, 18 * edge + row, 16 * edge + row - 2 * edge)
    wanted = jnp.where(row < 4 * edge, wanted, -2)
    outer = jnp.where(wanted == source, -0.5, 0.0).astype(BF16)
    halo_lift[...] = dot(outer, lift[...]).astype(BF16)
    row = lax.broadcasted_iota(jnp.int32, (256, 128), 0)
    col = lax.broadcasted_iota(jnp.int32, (256, 128), 1)
    chosen = jnp.full((256, 128), -1, jnp.int32)
    for s in range(4):
        chosen = jnp.where(col // edge == s, sides_ref[0, s] * edge + col % edge, chosen)
    pick[...] = dot(lift_t[...], jnp.where(row == chosen, 1.0, 0.0).astype(BF16)).astype(BF16)
    for e in range(elems):
        for g in range(elems):
            rows = slice(g * nodes, g * nodes + nodes)
            cols = slice(e * nodes, e * nodes + nodes)
            block = -0.5 * dot(lift_t[rows, :], inner[:, cols])
            if g == e:
                block = block + stiff[e].astype(F32)
            dense[rows, cols] = block.astype(BF16)
    for e in range(elems):
        for q in range(2):
            lanes = slice(128 * q, 128 * q + 128)
            even, odd = split(slope[e, 0, :, lanes].astype(F32), slope[e, 1, :, lanes].astype(F32))
            weights[e, :, 256 * q : 256 * q + 128] = even.astype(BF16)
            weights[e, :, 256 * q + 128 : 256 * q + 256] = odd.astype(BF16)

    tail = half + 16
    flux_c[tail:, :] = jnp.zeros((flux_c.shape[0] - tail, 256), BF16)

    for k in range(1, parts):
        peer = lax.rem(me + k, parts)
        pltpu.make_async_remote_copy(
            send1.at[peer],
            recv1.at[:, pl.ds(peer * mode_count, mode_count), :],
            send1_sem.at[peer],
            recv1_sem.at[peer],
            device_id=(peer, patch),
            device_id_type=MESH,
        ).wait()
    own.wait()

    element = me // (parts // elems)
    wet = jnp.where(element < live_ref[0], scale * scale, 0.0).astype(F32)
    for first, count in ((0, 512), (512, 512), (1024, 512), (1536, 16)):
        rows = slice(first, first + count)
        even = dot(out_table[0, rows, :], recv1[0])
        odd = dot(out_table[1, rows, :], recv1[1])
        mask = lax.broadcasted_iota(jnp.int32, (count, 128), 1) < 64
        flux = []
        for field in (even + odd, even - odd):
            last = field[:, 128:]
            turned = pltpu.roll(last, 64, 1)
            warm = jnp.where(mask, turned, last) * wet
            flux.append((field[:, :128] * warm, last * turned * wet))
        for pair in range(2):
            lanes = slice(128 * pair, 128 * pair + 128)
            flux_c[rows, lanes] = (flux[0][pair] + flux[1][pair]).astype(BF16)
            if count > 16:
                flux_s[rows, lanes] = (flux[0][pair] - flux[1][pair]).astype(BF16)
    even = dot(back_table[0], flux_c[...]) * scale
    odd = dot(back_table[1, :, :half], flux_s[...]) * scale
    mask = lax.broadcasted_iota(jnp.int32, (modes, 128), 1) < 64
    send2[0] = even[:, :128].astype(BF16)
    send2[1] = odd[:, :128].astype(BF16)
    send2[2] = jnp.where(mask, even[:, 128:], odd[:, 128:]).astype(BF16)

    mine = pl.ds(pl.multiple_of(me * 128, 128), 128)
    own = pltpu.make_async_copy(
        send2.at[:, pl.ds(me * mode_count, mode_count), :], recv2.at[:, :, mine], own_sem
    )
    own.start()
    flights = []
    for k in range(1, parts):
        peer = lax.rem(me + k, parts)
        flights.append(
            pltpu.make_async_remote_copy(
                send2.at[:, pl.ds(peer * mode_count, mode_count), :],
                recv2.at[:, :, mine],
                send2_sem.at[k],
                recv2_sem.at[k],
                device_id=(peer, patch),
                device_id_type=MESH,
            )
        )
        flights[-1].start()
    for flight in flights:
        flight.wait()
    own.wait()

    wave = (lax.broadcasted_iota(jnp.int32, (mode_count, 1), 0) + me * mode_count).astype(F32)
    wave = wave / modes
    rhs = []
    moved = [
        dot_nt(recv2[0:2, :, 512 * e : 512 * e + 512].reshape(2 * mode_count, 512), weights[e])
        for e in range(elems)
    ]
    moved = jnp.concatenate(moved, axis=1)
    around = [[], []]
    for t in range(ndev // 128):
        even = recv2[2, :, 256 * t : 256 * t + 128].astype(F32)
        odd = recv2[2, :, 256 * t + 128 : 256 * t + 256].astype(F32)
        cosine, sine = split(even, odd)
        around[0].append(-wave * sine)
        around[1].append(wave * cosine)
    around = jnp.concatenate([jnp.concatenate(a, axis=1) for a in around], axis=0)
    rhs = heat[...].reshape(2 * mode_count, ndev) - 0.5 * (moved + around)

    wave2 = jnp.concatenate([wave, wave], axis=0)
    lane = lax.broadcasted_iota(jnp.int32, (1, ndev), 1)
    a, b = lane // edge % edge, lane % edge
    faces = sum(jnp.where(hit, 0.5, 0.0) for hit in (a == 0, a == edge - 1, b == 0, b == edge - 1))
    factor = (1.0 + wave2 * wave2) + faces
    rows2 = 2 * mode_count
    theta, delta = (4.0, 3.0)
    sigma = theta / delta
    total = jnp.zeros_like(rhs)
    resid = rhs
    walk = resid / theta
    rho = 1.0 / sigma
    right_lane = lax.broadcasted_iota(jnp.int32, (rows2, 128), 1) < 2 * edge
    for step in range(STEPS):
        high = walk.astype(BF16)
        halves[:rows2, :] = high
        halves[rows2:, :] = (walk - high.astype(F32)).astype(BF16)
        traces[step] = dot(high, pick[...]).astype(BF16)
        flights = []
        for side, dest in enumerate((right, left)):
            flights.append(
                pltpu.make_async_remote_copy(
                    traces.at[step],
                    halo.at[step, side],
                    halo_send_sem.at[step, side],
                    halo_recv_sem.at[step, side],
                    device_id=(me, dest),
                    device_id_type=MESH,
                )
            )
            flights[-1].start()
        local = dot(halves[...], dense[...])
        image = factor * walk + local[:rows2] + local[rows2:]
        for flight in flights:
            flight.wait()
        outside = jnp.where(right_lane, halo[step, 1].astype(F32), halo[step, 0].astype(F32)).astype(BF16)
        image = image + dot(outside, halo_lift[...])
        total = total + walk
        resid = resid - image
        rho_new = 1.0 / (2.0 * sigma - rho)
        walk = rho_new * rho * walk + 2.0 * rho_new / delta * resid
        rho = rho_new
    result_ref[...] = (total + walk).reshape(2, mode_count, ndev)


def per_device(
    flow_speed,
    heat_state,
    planar_slope_matrices,
    conduction_matrices,
    adjacent_partners,
    opposite_direction_flags,
    interpatch_sides,
    liquid_cells,
):
    parts = lax.axis_size("mode")
    patches = lax.axis_size("patch")
    _, _, mode_count, ndev = flow_speed.shape
    elems, nodes, _ = conduction_matrices.shape
    edge = math.isqrt(nodes)
    modes = mode_count * parts
    points = 3 * modes
    rows = points // 2 + 128
    out_table, back_table = tables(modes, points, rows)
    lift = lift_table(elems, edge)
    sizes = (parts, patches, mode_count, ndev, elems, edge, points)
    smem = pl.BlockSpec(memory_space=pltpu.SMEM)
    hbm = pl.BlockSpec(memory_space=pl.ANY)
    vmem = pl.BlockSpec(memory_space=pltpu.VMEM)
    big = (
        flow_speed,
        heat_state,
        planar_slope_matrices,
        conduction_matrices,
        jnp.asarray(out_table),
        jnp.asarray(back_table),
        jnp.asarray(lift.astype(BF16)),
        jnp.asarray(lift.T.astype(BF16)),
    )
    return pl.pallas_call(
        functools.partial(kernel, sizes),
        out_shape=jax.ShapeDtypeStruct(heat_state.shape, F32),
        in_specs=[smem] * 4 + [hbm] * 8,
        out_specs=vmem,
        scratch_shapes=[pltpu.VMEM(a.shape, a.dtype) for a in big]
        + [
            pltpu.VMEM((parts, 2, mode_count, 256), BF16),
            pltpu.VMEM((2, modes, 256), BF16),
            pltpu.VMEM((rows, 256), BF16),
            pltpu.VMEM((points // 2, 256), BF16),
            pltpu.VMEM((3, modes, 128), BF16),
            pltpu.VMEM((3, mode_count, parts * 128), BF16),
            pltpu.VMEM((elems, nodes, 2 * nodes), BF16),
            pltpu.VMEM((ndev, ndev), BF16),
            pltpu.VMEM((ndev, 128), BF16),
            pltpu.VMEM((128, ndev), BF16),
            pltpu.VMEM((4 * mode_count, ndev), BF16),
            pltpu.VMEM((STEPS, 2 * mode_count, 128), BF16),
            pltpu.VMEM((STEPS, 2, 2 * mode_count, 128), BF16),
            pltpu.SemaphoreType.DMA((8,)),
            pltpu.SemaphoreType.DMA,
            pltpu.SemaphoreType.DMA((parts,)),
            pltpu.SemaphoreType.DMA((parts,)),
            pltpu.SemaphoreType.DMA((parts,)),
            pltpu.SemaphoreType.DMA((parts,)),
            pltpu.SemaphoreType.DMA((STEPS, 2)),
            pltpu.SemaphoreType.DMA((STEPS, 2)),
        ],
        compiler_params=pltpu.CompilerParams(
            collective_id=0, has_side_effects=True, vmem_limit_bytes=56 << 20
        ),
    )(adjacent_partners, opposite_direction_flags, interpatch_sides, liquid_cells, *big)


def solution(mesh):
    placed = (
        P(None, None, "mode", "patch"),
        P(None, "mode", "patch"),
        P("patch", None, None, None),
        P("patch", None, None),
        P("patch", None),
        P("patch", None),
        P("patch", None),
        P("patch"),
    )
    return jax.shard_map(
        per_device, mesh=mesh, in_specs=placed, out_specs=P(None, "mode", "patch"), check_vma=False
    )
```

time: 226 us -> 59.8 us (0.26)
  local copies, waits for them, and re-layouts: 84.4 us -> 1.89 us
  other arithmetic: 77.4 us -> 0 us
  Pallas kernels: 0 us -> 56.4 us
  starting transfers between devices: 29.6 us -> 0 us
  matrix products: 23.2 us -> 0 us
  waiting for transfers between devices: 7.95 us -> 0 us
    pallas_call x0 -> x1, Pallas kernels: none -> 56.4 us  [per_device(): pl.pallas_call(functools.partial(kernel, sizes), out_shape=jax.ShapeDtype...]
    another operation x4 -> x0, other arithmetic: 52.9 us -> none
    dot_general x6 -> x0, matrix products: 23.2 us -> none  [the longest x1 8.65 us: per_device(): jnp.einsum('fbz,cmz->fcmb', flux, table, preferred_element_type=jnp.float32)]
    reshape x11 -> x0, local copies, waits for them, and re-layouts: 17.9 us -> none  [the longest x3 6.31 us: apply_operator(): local = jnp.einsum('eol,eno->enl', v.reshape(elems, nodes, lanes), stiff,...]
    all_to_all x2 -> x0, starting transfers between devices: 16.6 us -> none  [the longest x1 9.37 us: per_device(): lax.all_to_all(sampled_quantity, 'mode', split_axis=3, concat_axis=2, til...]
    add x9 -> x0, local copies, waits for them, and re-layouts: 14.1 us -> none  [the longest x8 13.5 us: apply_operator(): lifted + jnp.concatenate([jumps[:, 2][:, :, None], middle_cols, jumps[:,...]
    ppermute x6 -> x0, starting transfers between devices: 13 us -> none  [the longest x3 13 us: with_halo(): lax.ppermute(head, axis, [((i + 1) % count, i) for i in range(count)])]
    unnamed x35 -> x1, local copies, waits for them, and re-layouts: 14.1 us -> 1.89 us
  transfers between devices with their start and end apart: 8 -> 0, of which waited for: 1 -> 0; matrix products, arithmetic and copies ran while one was open for 41% -> 0% of each run, Pallas kernels for 0% -> 0%
where the time goes in v1:
time: 59.8 us; the launch traced here: 58.9 us
  Pallas kernels  56.4 us (94%)
  local copies, waits for them, and re-layouts  1.89 us (3%)
  between operations  0.66 us (1%)
    pallas_call x1, Pallas kernels, per_device(): pl.pallas_call(functools.partial(kernel, sizes), out_shape=jax.ShapeDtype...  56.4 us
    unnamed x1, local copies, waits for them, and re-layouts  1.89 us

profile of v1, /device:TPU:6, one launch (start us, length us, event | category | flops | bytes accessed | tf_op | source)
XLA Modules:
  0.0 58.9 jit_solution(12471207156582472423)
XLA Ops:
  0.7 56.4 %shard_map.118 = f32[2,64,1024]{2,1,0:T(8,128)} custom-call(s32[4,4]{1,0:T(4,128)} %partners_ref.1, s32[4,4]{1,0:T(4,128)} %flags_ref.1, s32[1,4]{1,0:T(1,128)} %sides_ref.1, s32[1]{0:T(128)S(6)} %copy.14.live_ref, bf16[3,2,64,1024]{3,2,1,0:T(8,128)(2,1)} %flow_hbm.1, f32[2,64,1024]{2,1,0:T(8,128)} %heat_hbm.1, bf16[4,2,256,256]{3,2,1,0:T(8,128)(2,1)} %slope_hbm.1, ...), custom_call_target="tpu_custom_call" | custom-call | tf_op jit(solution)/shard_map/pallas_call | solution.py:377
  57.1 1.9 %copy.15 = f32[2,64,1024]{2,1,0:T(8,128)} copy(f32[2,64,1024]{2,1,0:T(8,128)} %shard_map.118) | data formatting | bytes 1048576

commit v2 on v1

--- a/solution.py
+++ b/solution.py
@@ -81,8 +81,9 @@
     weights,
     dense,
     pick,
-    halo_lift,
-    halves,
+    spread,
+    respond,
+    respond_in,
     traces,
     halo,
     load_sem,
@@ -93,6 +94,8 @@
     recv2_sem,
     halo_send_sem,
     halo_recv_sem,
+    respond_send_sem,
+    respond_recv_sem,
 ):
     parts, patches, mode_count, ndev, elems, edge, points = sizes
     modes = mode_count * parts
@@ -191,22 +194,66 @@
     row = lax.broadcasted_iota(jnp.int32, (128, 256), 0)
     wanted = jnp.where(row < 2 * edge, 18 * edge + row, 16 * edge + row - 2 * edge)
     wanted = jnp.where(row < 4 * edge, wanted, -2)
-    outer = jnp.where(wanted == source, -0.5, 0.0).astype(BF16)
-    halo_lift[...] = dot(outer, lift[...]).astype(BF16)
+    outer = jnp.where(wanted == source, 0.5, 0.0).astype(BF16)
     row = lax.broadcasted_iota(jnp.int32, (256, 128), 0)
     col = lax.broadcasted_iota(jnp.int32, (256, 128), 1)
     chosen = jnp.full((256, 128), -1, jnp.int32)
     for s in range(4):
         chosen = jnp.where(col // edge == s, sides_ref[0, s] * edge + col % edge, chosen)
-    pick[...] = dot(lift_t[...], jnp.where(row == chosen, 1.0, 0.0).astype(BF16)).astype(BF16)
+    chosen = jnp.where(row == chosen, 1.0, 0.0).astype(BF16)
+    same = lax.broadcasted_iota(jnp.int32, (nodes, nodes), 0) == lax.broadcasted_iota(
+        jnp.int32, (nodes, nodes), 1
+    )
+    lane_diag, row_diag = [], []
     for e in range(elems):
         for g in range(elems):
             rows = slice(g * nodes, g * nodes + nodes)
             cols = slice(e * nodes, e * nodes + nodes)
             block = -0.5 * dot(lift_t[rows, :], inner[:, cols])
             if g == e:
-                block = block + stiff[e].astype(F32)
+                full = stiff[e].astype(F32)
+                diagonal = jnp.where(same, full, 0.0)
+                lane_diag.append(jnp.sum(diagonal, axis=0, keepdims=True))
+                row_diag.append(jnp.sum(diagonal, axis=1, keepdims=True))
+                block = block + (full - diagonal)
             dense[rows, cols] = block.astype(BF16)
+
+    def own_factor(axis):
+        shape = (1, ndev) if axis else (ndev, 1)
+        node = lax.broadcasted_iota(jnp.int32, shape, axis)
+        a, b = node // edge % edge, node % edge
+        hits = (a == 0, a == edge - 1, b == 0, b == edge - 1)
+        return 1.0 + sum(jnp.where(hit, 0.5, 0.0) for hit in hits)
+
+    factor = own_factor(1) + jnp.concatenate(lane_diag, axis=1)
+    row_factor = own_factor(0) + jnp.concatenate(row_diag, axis=0)
+    trace = dot(lift_t[...], chosen)
+    pick[:, 0:128] = trace.astype(BF16)
+    trace = trace * row_factor + dot(dense[...], pick[:, 0:128])
+    pick[:, 128:256] = trace.astype(BF16)
+    trace = trace * row_factor + dot(dense[...], pick[:, 128:256])
+    pick[:, 256:384] = trace.astype(BF16)
+    lifted = dot(outer, lift[...])
+    spread[0:128, :] = lifted.astype(BF16)
+    respond[0] = dot(spread[0:128, :], pick[:, 0:128]).astype(BF16)
+    respond[1] = dot(spread[0:128, :], pick[:, 128:256]).astype(BF16)
+    answers = []
+    for side, dest in enumerate((right, left)):
+        answers.append(
+            pltpu.make_async_remote_copy(
+                respond,
+                respond_in.at[side],
+                respond_send_sem.at[side],
+                respond_recv_sem.at[side],
+                device_id=(me, dest),
+                device_id_type=MESH,
+            )
+        )
+        answers[-1].start()
+    lifted = lifted * factor + dot(spread[0:128, :], dense[...])
+    spread[128:256, :] = lifted.astype(BF16)
+    lifted = lifted * factor + dot(spread[128:256, :], dense[...])
+    spread[256:384, :] = lifted.astype(BF16)
     for e in range(elems):
         for q in range(2):
             lanes = slice(128 * q, 128 * q + 128)
@@ -295,49 +342,84 @@
     around = jnp.concatenate([jnp.concatenate(a, axis=1) for a in around], axis=0)
     rhs = heat[...].reshape(2 * mode_count, ndev) - 0.5 * (moved + around)
 
-    wave2 = jnp.concatenate([wave, wave], axis=0)
-    lane = lax.broadcasted_iota(jnp.int32, (1, ndev), 1)
-    a, b = lane // edge % edge, lane % edge
-    faces = sum(jnp.where(hit, 0.5, 0.0) for hit in (a == 0, a == edge - 1, b == 0, b == edge - 1))
-    factor = (1.0 + wave2 * wave2) + faces
-    rows2 = 2 * mode_count
     theta, delta = (4.0, 3.0)
     sigma = theta / delta
+    rho = 1.0 / sigma
+    keep, take = [], []
+    for step in range(STEPS):
+        rho_new = 1.0 / (2.0 * sigma - rho)
+        keep.append(rho_new * rho)
+        take.append(2.0 * rho_new / delta)
+        rho = rho_new
+    (a0, a1, a2), (b0, b1, b2) = keep, take
+    wave2 = jnp.concatenate([wave, wave], axis=0)
+    wave2 = wave2 * wave2
+    powers = dot(rhs.astype(BF16), pick[...])
+    p0, p1, p2 = powers[:, 0:128], powers[:, 128:256], powers[:, 256:384]
+    once = wave2 * p0 + p1
+    twice = wave2 * once + wave2 * p1 + p2
+    t0 = p0 / theta
+    r1 = p0 - once / theta
+    t1 = a0 * t0 + b0 * r1
+    t2 = a1 * t1 + b1 * (r1 - ((a0 / theta + b0) * once - (b0 / theta) * twice))
+    traces[0] = t0.astype(BF16)
+    traces[1] = t1.astype(BF16)
+    traces[2] = t2.astype(BF16)
+    flights = []
+    for side, dest in enumerate((right, left)):
+        flights.append(
+            pltpu.make_async_remote_copy(
+                traces,
+                halo.at[side],
+                halo_send_sem.at[side],
+                halo_recv_sem.at[side],
+                device_id=(me, dest),
+                device_id_type=MESH,
+            )
+        )
+        flights[-1].start()
+
+    every = wave2 + factor
     total = jnp.zeros_like(rhs)
     resid = rhs
     walk = resid / theta
-    rho = 1.0 / sigma
-    right_lane = lax.broadcasted_iota(jnp.int32, (rows2, 128), 1) < 2 * edge
     for step in range(STEPS):
-        high = walk.astype(BF16)
-        halves[:rows2, :] = high
-        halves[rows2:, :] = (walk - high.astype(F32)).astype(BF16)
-        traces[step] = dot(high, pick[...]).astype(BF16)
-        flights = []
-        for side, dest in enumerate((right, left)):
-            flights.append(
-                pltpu.make_async_remote_copy(
-                    traces.at[step],
-                    halo.at[step, side],
-                    halo_send_sem.at[step, side],
-                    halo_recv_sem.at[step, side],
-                    device_id=(me, dest),
-                    device_id_type=MESH,
-                )
-            )
-            flights[-1].start()
-        local = dot(halves[...], dense[...])
-        image = factor * walk + local[:rows2] + local[rows2:]
-        for flight in flights:
-            flight.wait()
-        outside = jnp.where(right_lane, halo[step, 1].astype(F32), halo[step, 0].astype(F32)).astype(BF16)
-        image = image + dot(outside, halo_lift[...])
+        image = every * walk + dot(walk.astype(BF16), dense[...])
         total = total + walk
         resid = resid - image
-        rho_new = 1.0 / (2.0 * sigma - rho)
-        walk = rho_new * rho * walk + 2.0 * rho_new / delta * resid
-        rho = rho_new
+        walk = keep[step] * walk + take[step] * resid
     result_ref[...] = (total + walk).reshape(2, mode_count, ndev)
+
+    for answer in answers:
+        answer.wait()
+    below = lax.broadcasted_iota(jnp.int32, (128, 128), 0) < 2 * edge
+    reply0 = jnp.where(below, respond_in[0, 0].astype(F32), respond_in[1, 0].astype(F32)).astype(BF16)
+    reply1 = jnp.where(below, respond_in[0, 1].astype(F32), respond_in[1, 1].astype(F32)).astype(BF16)
+    back0 = dot(traces[0], reply0)
+    back1 = dot(traces[1], reply0)
+    back00 = dot(traces[0], reply1)
+    around0 = dot(respond[0], reply0).astype(BF16)
+
+    for flight in flights:
+        flight.wait()
+    mine = lax.broadcasted_iota(jnp.int32, (2 * mode_count, 128), 1) < 2 * edge
+    s0, s1, s2 = [
+        jnp.where(mine, halo[1, step].astype(F32), halo[0, step].astype(F32))
+        for step in range(STEPS)
+    ]
+    back1 = back1 + b0 * dot(s0.astype(BF16), around0)
+    s1 = s1 + b0 * back0
+    first = 1.0 - b0 * wave2
+    s2 = s2 + (a1 * b0 + b1 * first) * back0 + b1 * (back1 - b0 * back00)
+    grown = first * s0 + s1
+    alpha = a1 * b0 * s0 + b1 * grown
+    beta = -b1 * b0 * s0
+    y0 = b0 * s0 + (1.0 + a2) * alpha + b2 * (grown - wave2 * alpha + s2)
+    y1 = (1.0 + a2) * beta + b2 * (-b0 * s0 - wave2 * beta - alpha)
+    y2 = -b2 * beta
+    y = jnp.concatenate([y0.astype(BF16), y1.astype(BF16), y2.astype(BF16)], axis=1)
+    outside = dot(y, spread[...])
+    result_ref[...] = result_ref[...] + outside.reshape(2, mode_count, ndev)
 
 
 def per_device(
@@ -389,19 +471,22 @@
             pltpu.VMEM((3, mode_count, parts * 128), BF16),
             pltpu.VMEM((elems, nodes, 2 * nodes), BF16),
             pltpu.VMEM((ndev, ndev), BF16),
-            pltpu.VMEM((ndev, 128), BF16),
-            pltpu.VMEM((128, ndev), BF16),
-            pltpu.VMEM((4 * mode_count, ndev), BF16),
+            pltpu.VMEM((ndev, STEPS * 128), BF16),
+            pltpu.VMEM((STEPS * 128, ndev), BF16),
+            pltpu.VMEM((2, 128, 128), BF16),
+            pltpu.VMEM((2, 2, 128, 128), BF16),
             pltpu.VMEM((STEPS, 2 * mode_count, 128), BF16),
-            pltpu.VMEM((STEPS, 2, 2 * mode_count, 128), BF16),
+            pltpu.VMEM((2, STEPS, 2 * mode_count, 128), BF16),
             pltpu.SemaphoreType.DMA((8,)),
             pltpu.SemaphoreType.DMA,
             pltpu.SemaphoreType.DMA((parts,)),
             pltpu.SemaphoreType.DMA((parts,)),
             pltpu.SemaphoreType.DMA((parts,)),
             pltpu.SemaphoreType.DMA((parts,)),
-            pltpu.SemaphoreType.DMA((STEPS, 2)),
-            pltpu.SemaphoreType.DMA((STEPS, 2)),
+            pltpu.SemaphoreType.DMA((2,)),
+            pltpu.SemaphoreType.DMA((2,)),
+            pltpu.SemaphoreType.DMA((2,)),
+            pltpu.SemaphoreType.DMA((2,)),
         ],
         compiler_params=pltpu.CompilerParams(
             collective_id=0, has_side_effects=True, vmem_limit_bytes=56 << 20

time: 59.8 us -> 53.2 us (0.89)
  Pallas kernels: 56.4 us -> 49.8 us
    pallas_call x1, Pallas kernels: 56.4 us -> 49.8 us  [per_device(): pl.pallas_call(functools.partial(kernel, sizes), out_shape=jax.ShapeDtype...]
where the time goes in v2:
time: 53.2 us; the launch traced here: 52.4 us
  Pallas kernels  49.8 us (94%)
  local copies, waits for them, and re-layouts  1.89 us (4%)
  between operations  0.66 us (1%)
    pallas_call x1, Pallas kernels, per_device(): pl.pallas_call(functools.partial(kernel, sizes), out_shape=jax.ShapeDtype...  49.8 us
    unnamed x1, local copies, waits for them, and re-layouts  1.89 us

profile of v2, /device:TPU:6, one launch (start us, length us, event | category | flops | bytes accessed | tf_op | source)
XLA Modules:
  0.0 52.4 jit_solution(12339125418266320678)
XLA Ops:
  0.7 49.8 %shard_map.118 = f32[2,64,1024]{2,1,0:T(8,128)} custom-call(s32[4,4]{1,0:T(4,128)} %partners_ref.1, s32[4,4]{1,0:T(4,128)} %flags_ref.1, s32[1,4]{1,0:T(1,128)} %sides_ref.1, s32[1]{0:T(128)S(6)} %copy.14.live_ref, bf16[3,2,64,1024]{3,2,1,0:T(8,128)(2,1)} %flow_hbm.1, f32[2,64,1024]{2,1,0:T(8,128)} %heat_hbm.1, bf16[4,2,256,256]{3,2,1,0:T(8,128)(2,1)} %slope_hbm.1, ...), custom_call_target="tpu_custom_call" | custom-call | tf_op jit(solution)/shard_map/pallas_call | solution.py:459
  50.5 1.9 %copy.15 = f32[2,64,1024]{2,1,0:T(8,128)} copy(f32[2,64,1024]{2,1,0:T(8,128)} %shard_map.118) | data formatting | bytes 1048576

commit v3 on v2

--- a/solution.py
+++ b/solution.py
@@ -10,6 +10,7 @@
 from jax.sharding import PartitionSpec as P
 
 STEPS = 3
+ORDER = (2, 1, 3, 0)
 MESH = pl.DeviceIdType.MESH
 F32 = jnp.float32
 BF16 = jnp.bfloat16
@@ -51,10 +52,10 @@
 
 def kernel(
     sizes,
-    partners_ref,
-    flags_ref,
-    sides_ref,
     live_ref,
+    partners_hbm,
+    flags_hbm,
+    sides_hbm,
     flow_hbm,
     heat_hbm,
     slope_hbm,
@@ -64,6 +65,9 @@
     lift_hbm,
     lift_t_hbm,
     result_ref,
+    partners_ref,
+    flags_ref,
+    sides_ref,
     flow,
     heat,
     slope,
@@ -74,11 +78,13 @@
     lift_t,
     send1,
     recv1,
+    phys,
     flux_c,
     flux_s,
     send2,
     recv2,
     weights,
+    forcing,
     dense,
     pick,
     spread,
@@ -119,6 +125,9 @@
                 (stiff_hbm, stiff),
                 (lift_hbm, lift),
                 (lift_t_hbm, lift_t),
+                (partners_hbm, partners_ref),
+                (flags_hbm, flags_ref),
+                (sides_hbm, sides_ref),
             )
         )
     ]
@@ -132,8 +141,6 @@
         )
     for side in (left, right):
         pl.semaphore_signal(barrier, inc=1, device_id=(me, side), device_id_type=MESH)
-
-    low = lax.broadcasted_iota(jnp.int32, (mode_count, 128), 1) < 64
 
     def split(a, b):
         mask = lax.broadcasted_iota(jnp.int32, a.shape, 1) < 64
@@ -144,38 +151,39 @@
 
     loads[0].wait()
     loads[1].wait()
-    barred = False
-    for step in range(parts // 2):
-        tile = lax.rem(me // 2 + step, parts // 2)
-        cols = pl.ds(pl.multiple_of(tile * 128, 128), 128)
-        for c in range(2):
-            fields = [flow[f, c, :, cols].astype(F32) for f in range(3)]
-            fields.append(heat[c, :, cols].astype(BF16).astype(F32))
-            for pair in range(2):
-                even, odd = split(fields[2 * pair], fields[2 * pair + 1])
-                lanes = slice(128 * pair, 128 * pair + 128)
-                send1[2 * tile, c, :, lanes] = even.astype(BF16)
-                send1[2 * tile + 1, c, :, lanes] = odd.astype(BF16)
-        if not barred:
+    ring = parts // elems
+    home, place = me // ring, lax.rem(me, ring)
+
+    def mates(quarter):
+        return [quarter * ring + lax.rem(place + k, ring) for k in range(1, ring + 1)]
+
+    my_rows = pl.ds(pl.multiple_of(me * mode_count, mode_count), mode_count)
+    for turn in ORDER:
+        quarter = lax.rem(home + turn, elems)
+        for half_tile in range(2):
+            tile = 2 * quarter + half_tile
+            cols = pl.ds(pl.multiple_of(tile * 128, 128), 128)
+            for c in range(2):
+                fields = [flow[f, c, :, cols].astype(F32) for f in range(3)]
+                fields.append(heat[c, :, cols].astype(BF16).astype(F32))
+                for pair in range(2):
+                    even, odd = split(fields[2 * pair], fields[2 * pair + 1])
+                    lanes = slice(128 * pair, 128 * pair + 128)
+                    send1[2 * tile, c, :, lanes] = even.astype(BF16)
+                    send1[2 * tile + 1, c, :, lanes] = odd.astype(BF16)
+        if turn == ORDER[0]:
             pl.semaphore_wait(barrier, parts + 1)
-            barred = True
-            own = pltpu.make_async_copy(
-                send1.at[me], recv1.at[:, pl.ds(me * mode_count, mode_count), :], own_sem
-            )
-            own.start()
-            other = lax.rem(me, 2)
-            dests = [2 * tile + 1 - other]
-        else:
-            dests = [2 * tile, 2 * tile + 1]
-        for dest in dests:
+        for dest in mates(quarter)[: ring if turn else ring - 1]:
             pltpu.make_async_remote_copy(
                 send1.at[dest],
-                recv1.at[:, pl.ds(me * mode_count, mode_count), :],
+                recv1.at[:, my_rows, :],
                 send1_sem.at[dest],
                 recv1_sem.at[me],
                 device_id=(dest, patch),
                 device_id_type=MESH,
             ).start()
+    own = pltpu.make_async_copy(send1.at[me], recv1.at[:, my_rows, :], own_sem)
+    own.start()
 
     for load in loads[2:]:
         load.wait()
@@ -264,83 +272,105 @@
     tail = half + 16
     flux_c[tail:, :] = jnp.zeros((flux_c.shape[0] - tail, 256), BF16)
 
-    for k in range(1, parts):
-        peer = lax.rem(me + k, parts)
-        pltpu.make_async_remote_copy(
+    def flight1(peer):
+        rows = pl.ds(pl.multiple_of(peer * mode_count, mode_count), mode_count)
+        return pltpu.make_async_remote_copy(
             send1.at[peer],
-            recv1.at[:, pl.ds(peer * mode_count, mode_count), :],
+            recv1.at[:, rows, :],
             send1_sem.at[peer],
             recv1_sem.at[peer],
             device_id=(peer, patch),
             device_id_type=MESH,
-        ).wait()
-    own.wait()
-
-    element = me // (parts // elems)
-    wet = jnp.where(element < live_ref[0], scale * scale, 0.0).astype(F32)
-    for first, count in ((0, 512), (512, 512), (1024, 512), (1536, 16)):
-        rows = slice(first, first + count)
-        even = dot(out_table[0, rows, :], recv1[0])
-        odd = dot(out_table[1, rows, :], recv1[1])
-        mask = lax.broadcasted_iota(jnp.int32, (count, 128), 1) < 64
-        flux = []
-        for field in (even + odd, even - odd):
-            last = field[:, 128:]
-            turned = pltpu.roll(last, 64, 1)
-            warm = jnp.where(mask, turned, last) * wet
-            flux.append((field[:, :128] * warm, last * turned * wet))
-        for pair in range(2):
-            lanes = slice(128 * pair, 128 * pair + 128)
-            flux_c[rows, lanes] = (flux[0][pair] + flux[1][pair]).astype(BF16)
-            if count > 16:
-                flux_s[rows, lanes] = (flux[0][pair] - flux[1][pair]).astype(BF16)
-    even = dot(back_table[0], flux_c[...]) * scale
-    odd = dot(back_table[1, :, :half], flux_s[...]) * scale
-    mask = lax.broadcasted_iota(jnp.int32, (modes, 128), 1) < 64
-    send2[0] = even[:, :128].astype(BF16)
-    send2[1] = odd[:, :128].astype(BF16)
-    send2[2] = jnp.where(mask, even[:, 128:], odd[:, 128:]).astype(BF16)
-
-    mine = pl.ds(pl.multiple_of(me * 128, 128), 128)
-    own = pltpu.make_async_copy(
-        send2.at[:, pl.ds(me * mode_count, mode_count), :], recv2.at[:, :, mine], own_sem
-    )
+        )
+
+    wet = jnp.where(home < live_ref[0, 0], scale * scale, 0.0).astype(F32)
+    span = ring * mode_count
+    for turn in ORDER:
+        quarter = lax.rem(home + elems - turn, elems)
+        for source in mates(quarter)[: ring if turn else ring - 1]:
+            flight1(source).wait_recv()
+        if turn == 0:
+            own.wait()
+        depth = pl.ds(pl.multiple_of(quarter * span, span), span)
+        for first, count in ((0, 512), (512, 512), (1024, 512), (1536, 16)):
+            rows = slice(first, first + count)
+            even = dot(out_table[0, rows, depth], recv1[0, depth, :])
+            odd = dot(out_table[1, rows, depth], recv1[1, depth, :])
+            if turn != ORDER[0]:
+                even = even + phys[0, rows, :]
+                odd = odd + phys[1, rows, :]
+            if turn != ORDER[-1]:
+                phys[0, rows, :] = even
+                phys[1, rows, :] = odd
+                continue
+            mask = lax.broadcasted_iota(jnp.int32, (count, 128), 1) < 64
+            flux = []
+            for field in (even + odd, even - odd):
+                last = field[:, 128:]
+                turned = pltpu.roll(last, 64, 1)
+                warm = jnp.where(mask, turned, last) * wet
+                flux.append((field[:, :128] * warm, last * turned * wet))
+            for pair in range(2):
+                lanes = slice(128 * pair, 128 * pair + 128)
+                flux_c[rows, lanes] = (flux[0][pair] + flux[1][pair]).astype(BF16)
+                if count > 16:
+                    flux_s[rows, lanes] = (flux[0][pair] - flux[1][pair]).astype(BF16)
+
+    my_lanes = pl.ds(pl.multiple_of(me * 128, 128), 128)
+
+    def flight2(peer, incoming):
+        rows = pl.ds(pl.multiple_of(peer * mode_count, mode_count), mode_count)
+        return pltpu.make_async_remote_copy(
+            send2.at[:, rows, :],
+            recv2.at[:, :, my_lanes],
+            send2_sem.at[peer],
+            recv2_sem.at[incoming],
+            device_id=(peer, patch),
+            device_id_type=MESH,
+        )
+
+    mask = lax.broadcasted_iota(jnp.int32, (span, 128), 1) < 64
+    for turn in ORDER:
+        quarter = lax.rem(home + turn, elems)
+        rows = pl.ds(pl.multiple_of(quarter * span, span), span)
+        even = dot(back_table[0, rows, :], flux_c[...]) * scale
+        odd = dot(back_table[1, rows, :half], flux_s[...]) * scale
+        send2[0, rows, :] = even[:, :128].astype(BF16)
+        send2[1, rows, :] = odd[:, :128].astype(BF16)
+        send2[2, rows, :] = jnp.where(mask, even[:, 128:], odd[:, 128:]).astype(BF16)
+        for dest in mates(quarter)[: ring if turn else ring - 1]:
+            flight2(dest, me).start()
+    own = pltpu.make_async_copy(send2.at[:, my_rows, :], recv2.at[:, :, my_lanes], own_sem)
     own.start()
-    flights = []
     for k in range(1, parts):
-        peer = lax.rem(me + k, parts)
-        flights.append(
-            pltpu.make_async_remote_copy(
-                send2.at[:, pl.ds(peer * mode_count, mode_count), :],
-                recv2.at[:, :, mine],
-                send2_sem.at[k],
-                recv2_sem.at[k],
-                device_id=(peer, patch),
-                device_id_type=MESH,
-            )
-        )
-        flights[-1].start()
-    for flight in flights:
-        flight.wait()
-    own.wait()
+        flight1(lax.rem(me + k, parts)).wait_send()
 
     wave = (lax.broadcasted_iota(jnp.int32, (mode_count, 1), 0) + me * mode_count).astype(F32)
     wave = wave / modes
-    rhs = []
-    moved = [
-        dot_nt(recv2[0:2, :, 512 * e : 512 * e + 512].reshape(2 * mode_count, 512), weights[e])
-        for e in range(elems)
-    ]
-    moved = jnp.concatenate(moved, axis=1)
-    around = [[], []]
-    for t in range(ndev // 128):
-        even = recv2[2, :, 256 * t : 256 * t + 128].astype(F32)
-        odd = recv2[2, :, 256 * t + 128 : 256 * t + 256].astype(F32)
-        cosine, sine = split(even, odd)
-        around[0].append(-wave * sine)
-        around[1].append(wave * cosine)
-    around = jnp.concatenate([jnp.concatenate(a, axis=1) for a in around], axis=0)
-    rhs = heat[...].reshape(2 * mode_count, ndev) - 0.5 * (moved + around)
+    powers = jnp.zeros((2 * mode_count, STEPS * 128), F32)
+    for turn in ORDER:
+        quarter = lax.rem(home + elems - turn, elems)
+        for source in mates(quarter)[: ring if turn else ring - 1]:
+            flight2(source, source).wait_recv()
+        if turn == 0:
+            own.wait()
+        depth = pl.ds(pl.multiple_of(quarter * 2 * nodes, 2 * nodes), 2 * nodes)
+        moved = dot_nt(
+            recv2[0:2, :, depth].reshape(2 * mode_count, 2 * nodes), weights[quarter]
+        )
+        around = [[], []]
+        for t in range(2):
+            first = quarter * 2 * nodes + 256 * t
+            even = recv2[2, :, pl.ds(pl.multiple_of(first, 128), 128)].astype(F32)
+            odd = recv2[2, :, pl.ds(pl.multiple_of(first + 128, 128), 128)].astype(F32)
+            cosine, sine = split(even, odd)
+            around[0].append(-wave * sine)
+            around[1].append(wave * cosine)
+        around = jnp.concatenate([jnp.concatenate(a, axis=1) for a in around], axis=0)
+        lanes = pl.ds(pl.multiple_of(quarter * nodes, nodes), nodes)
+        part = heat[:, :, lanes].reshape(2 * mode_count, nodes) - 0.5 * (moved + around)
+        forcing[:, lanes] = part
+        powers = powers + dot(part.astype(BF16), pick[lanes, :])
 
     theta, delta = (4.0, 3.0)
     sigma = theta / delta
@@ -354,7 +384,6 @@
     (a0, a1, a2), (b0, b1, b2) = keep, take
     wave2 = jnp.concatenate([wave, wave], axis=0)
     wave2 = wave2 * wave2
-    powers = dot(rhs.astype(BF16), pick[...])
     p0, p1, p2 = powers[:, 0:128], powers[:, 128:256], powers[:, 256:384]
     once = wave2 * p0 + p1
     twice = wave2 * once + wave2 * p1 + p2
@@ -379,6 +408,7 @@
         )
         flights[-1].start()
 
+    rhs = forcing[...]
     every = wave2 + factor
     total = jnp.zeros_like(rhs)
     resid = rhs
@@ -400,6 +430,9 @@
     back00 = dot(traces[0], reply1)
     around0 = dot(respond[0], reply0).astype(BF16)
 
+    for k in range(1, parts):
+        peer = lax.rem(me + k, parts)
+        flight2(peer, peer).wait_send()
     for flight in flights:
         flight.wait()
     mine = lax.broadcasted_iota(jnp.int32, (2 * mode_count, 128), 1) < 2 * edge
@@ -420,6 +453,12 @@
     y = jnp.concatenate([y0.astype(BF16), y1.astype(BF16), y2.astype(BF16)], axis=1)
     outside = dot(y, spread[...])
     result_ref[...] = result_ref[...] + outside.reshape(2, mode_count, ndev)
+
+
+def hand_over(solved_ref, result_ref, sem):
+    copy = pltpu.make_async_copy(solved_ref, result_ref, sem)
+    copy.start()
+    copy.wait()
 
 
 def per_device(
@@ -443,9 +482,9 @@
     out_table, back_table = tables(modes, points, rows)
     lift = lift_table(elems, edge)
     sizes = (parts, patches, mode_count, ndev, elems, edge, points)
-    smem = pl.BlockSpec(memory_space=pltpu.SMEM)
-    hbm = pl.BlockSpec(memory_space=pl.ANY)
+    hbm = pl.BlockSpec(memory_space=pltpu.HBM)
     vmem = pl.BlockSpec(memory_space=pltpu.VMEM)
+    small = (adjacent_partners, opposite_direction_flags, interpatch_sides)
     big = (
         flow_speed,
         heat_state,
@@ -456,20 +495,23 @@
         jnp.asarray(lift.astype(BF16)),
         jnp.asarray(lift.T.astype(BF16)),
     )
-    return pl.pallas_call(
+    solved = pl.pallas_call(
         functools.partial(kernel, sizes),
-        out_shape=jax.ShapeDtypeStruct(heat_state.shape, F32),
-        in_specs=[smem] * 4 + [hbm] * 8,
+        out_shape=pltpu.VMEM(heat_state.shape, F32),
+        in_specs=[pl.BlockSpec(memory_space=pltpu.SMEM)] + [hbm] * 11,
         out_specs=vmem,
-        scratch_shapes=[pltpu.VMEM(a.shape, a.dtype) for a in big]
+        scratch_shapes=[pltpu.SMEM(a.shape, a.dtype) for a in small]
+        + [pltpu.VMEM(a.shape, a.dtype) for a in big]
         + [
             pltpu.VMEM((parts, 2, mode_count, 256), BF16),
             pltpu.VMEM((2, modes, 256), BF16),
+            pltpu.VMEM((2, points // 2 + 16, 256), F32),
             pltpu.VMEM((rows, 256), BF16),
             pltpu.VMEM((points // 2, 256), BF16),
             pltpu.VMEM((3, modes, 128), BF16),
             pltpu.VMEM((3, mode_count, parts * 128), BF16),
             pltpu.VMEM((elems, nodes, 2 * nodes), BF16),
+            pltpu.VMEM((2 * mode_count, ndev), F32),
             pltpu.VMEM((ndev, ndev), BF16),
             pltpu.VMEM((ndev, STEPS * 128), BF16),
             pltpu.VMEM((STEPS * 128, ndev), BF16),
@@ -477,7 +519,7 @@
             pltpu.VMEM((2, 2, 128, 128), BF16),
             pltpu.VMEM((STEPS, 2 * mode_count, 128), BF16),
             pltpu.VMEM((2, STEPS, 2 * mode_count, 128), BF16),
-            pltpu.SemaphoreType.DMA((8,)),
+            pltpu.SemaphoreType.DMA((11,)),
             pltpu.SemaphoreType.DMA,
             pltpu.SemaphoreType.DMA((parts,)),
             pltpu.SemaphoreType.DMA((parts,)),
@@ -489,9 +531,20 @@
             pltpu.SemaphoreType.DMA((2,)),
         ],
         compiler_params=pltpu.CompilerParams(
-            collective_id=0, has_side_effects=True, vmem_limit_bytes=56 << 20
+            collective_id=0, has_side_effects=True, vmem_limit_bytes=52 << 20
         ),
-    )(adjacent_partners, opposite_direction_flags, interpatch_sides, liquid_cells, *big)
+    )(
+        liquid_cells.reshape(1, 1),
+        *[pltpu.with_memory_space_constraint(a, pltpu.HBM) for a in small + big],
+    )
+    return pl.pallas_call(
+        hand_over,
+        out_shape=jax.ShapeDtypeStruct(heat_state.shape, F32),
+        in_specs=[vmem],
+        out_specs=hbm,
+        scratch_shapes=[pltpu.SemaphoreType.DMA],
+        compiler_params=pltpu.CompilerParams(vmem_limit_bytes=4 << 20),
+    )(solved)
 
 
 def solution(mesh):

time: 53.2 us -> 47.4 us (0.89); the launches traced: 52.4 us -> 47.2 us
  Pallas kernels: 49.8 us -> 46.6 us
  local copies, waits for them, and re-layouts: 1.89 us -> 0 us
    pallas_call x1 -> x2, Pallas kernels: 49.8 us -> 46.6 us  [the longest x1 45.8 us: per_device(): pl.pallas_call(functools.partial(kernel, sizes), out_shape=pltpu.VMEM(hea...]
    unnamed x1 -> x0, local copies, waits for them, and re-layouts: 1.89 us -> none
where the time goes in v3:
time: 47.4 us; the launch traced here: 47.2 us
  Pallas kernels  46.6 us (98%)
  between operations  0.66 us (1%)
    pallas_call x1, Pallas kernels, per_device(): pl.pallas_call(functools.partial(kernel, sizes), out_shape=pltpu.VMEM(hea...  45.8 us

profile of v3, /device:TPU:6, one launch (start us, length us, event | category | flops | bytes accessed | tf_op | source)
XLA Modules:
  0.0 47.2 jit_solution(16742018885535712360)
XLA Ops:
  0.7 45.8 %shard_map.118.solved_ref = f32[2,64,1024]{2,1,0:T(8,128)S(1)} custom-call(s32[1,1]{1,0:T(1,128)} %bitcast.1.live_ref, s32[4,4]{1,0:T(4,128)} %partners_hbm.1, s32[4,4]{1,0:T(4,128)} %flags_hbm.1, s32[1,4]{1,0:T(1,128)} %sides_hbm.1, bf16[3,2,64,1024]{3,2,1,0:T(8,128)(2,1)} %flow_hbm.1, f32[2,64,1024]{2,1,0:T(8,128)} %heat_hbm.1, ...), custom_call_target="tpu_custom_call" | custom-call | tf_op jit(solution)/shard_map/pallas_call | solution.py:498
  46.4 0.8 %shard_map.119 = f32[2,64,1024]{2,1,0:T(8,128)} custom-call(f32[2,64,1024]{2,1,0:T(8,128)S(1)} %shard_map.118.solved_ref), custom_call_target="tpu_custom_call" | custom-call | tf_op jit(solution)/shard_map/pallas_call | solution.py:540

commit v4 on v3

--- a/solution.py
+++ b/solution.py
@@ -11,6 +11,7 @@
 
 STEPS = 3
 ORDER = (2, 1, 3, 0)
+BACK_ORDER = (1, 3, 2, 0)
 MESH = pl.DeviceIdType.MESH
 F32 = jnp.float32
 BF16 = jnp.bfloat16
@@ -79,12 +80,14 @@
     send1,
     recv1,
     phys,
+    warm,
     flux_c,
     flux_s,
     send2,
     recv2,
     weights,
     forcing,
+    applied,
     dense,
     pick,
     spread,
@@ -131,7 +134,7 @@
             )
         )
     ]
-    for load in loads:
+    for load in loads[:2]:
         load.start()
 
     barrier = pltpu.get_barrier_semaphore()
@@ -151,6 +154,8 @@
 
     loads[0].wait()
     loads[1].wait()
+    for load in loads[2:]:
+        load.start()
     ring = parts // elems
     home, place = me // ring, lax.rem(me, ring)
 
@@ -158,32 +163,39 @@
         return [quarter * ring + lax.rem(place + k, ring) for k in range(1, ring + 1)]
 
     my_rows = pl.ds(pl.multiple_of(me * mode_count, mode_count), mode_count)
-    for turn in ORDER:
-        quarter = lax.rem(home + turn, elems)
-        for half_tile in range(2):
-            tile = 2 * quarter + half_tile
-            cols = pl.ds(pl.multiple_of(tile * 128, 128), 128)
-            for c in range(2):
-                fields = [flow[f, c, :, cols].astype(F32) for f in range(3)]
-                fields.append(heat[c, :, cols].astype(BF16).astype(F32))
-                for pair in range(2):
-                    even, odd = split(fields[2 * pair], fields[2 * pair + 1])
-                    lanes = slice(128 * pair, 128 * pair + 128)
-                    send1[2 * tile, c, :, lanes] = even.astype(BF16)
-                    send1[2 * tile + 1, c, :, lanes] = odd.astype(BF16)
-        if turn == ORDER[0]:
-            pl.semaphore_wait(barrier, parts + 1)
-        for dest in mates(quarter)[: ring if turn else ring - 1]:
-            pltpu.make_async_remote_copy(
-                send1.at[dest],
-                recv1.at[:, my_rows, :],
-                send1_sem.at[dest],
-                recv1_sem.at[me],
-                device_id=(dest, patch),
-                device_id_type=MESH,
-            ).start()
-    own = pltpu.make_async_copy(send1.at[me], recv1.at[:, my_rows, :], own_sem)
-    own.start()
+    owns = []
+    for pair in (1, 0):
+        lanes = slice(128 * pair, 128 * pair + 128)
+        for turn in ORDER:
+            quarter = lax.rem(home + turn, elems)
+            for half_tile in range(2):
+                tile = 2 * quarter + half_tile
+                cols = pl.ds(pl.multiple_of(tile * 128, 128), 128)
+                for c in range(2):
+                    first = flow[2 * pair, c, :, cols].astype(F32)
+                    if pair:
+                        second = heat[c, :, cols].astype(BF16).astype(F32)
+                    else:
+                        second = flow[1, c, :, cols].astype(F32)
+                    even, odd = split(first, second)
+                    send1[2 * tile, pair, c] = even.astype(BF16)
+                    send1[2 * tile + 1, pair, c] = odd.astype(BF16)
+            if pair and turn == ORDER[0]:
+                pl.semaphore_wait(barrier, parts + 1)
+            for dest in mates(quarter)[: ring if turn else ring - 1]:
+                pltpu.make_async_remote_copy(
+                    send1.at[dest, pair],
+                    recv1.at[pair, :, my_rows, :],
+                    send1_sem.at[pair, dest],
+                    recv1_sem.at[pair, me],
+                    device_id=(dest, patch),
+                    device_id_type=MESH,
+                ).start()
+        own = pltpu.make_async_copy(
+            send1.at[me, pair], recv1.at[pair, :, my_rows, :], own_sem.at[pair]
+        )
+        own.start()
+        owns.insert(0, own)
 
     for load in loads[2:]:
         load.wait()
@@ -272,107 +284,115 @@
     tail = half + 16
     flux_c[tail:, :] = jnp.zeros((flux_c.shape[0] - tail, 256), BF16)
 
-    def flight1(peer):
+    def flight1(peer, pair):
         rows = pl.ds(pl.multiple_of(peer * mode_count, mode_count), mode_count)
         return pltpu.make_async_remote_copy(
-            send1.at[peer],
-            recv1.at[:, rows, :],
-            send1_sem.at[peer],
-            recv1_sem.at[peer],
+            send1.at[peer, pair],
+            recv1.at[pair, :, rows, :],
+            send1_sem.at[pair, peer],
+            recv1_sem.at[pair, peer],
             device_id=(peer, patch),
             device_id_type=MESH,
         )
 
+    def flight2(peer, incoming, pair):
+        rows = pl.ds(pl.multiple_of(peer * mode_count, mode_count), mode_count)
+        planes = pl.ds(2 * pair, 2 - pair)
+        return pltpu.make_async_remote_copy(
+            send2.at[planes, rows, :],
+            recv2.at[me, planes],
+            send2_sem.at[pair, peer],
+            recv2_sem.at[pair, incoming],
+            device_id=(peer, patch),
+            device_id_type=MESH,
+        )
+
     wet = jnp.where(home < live_ref[0, 0], scale * scale, 0.0).astype(F32)
     span = ring * mode_count
-    for turn in ORDER:
+    for pair in (1, 0):
+        lanes = slice(128 * pair, 128 * pair + 128)
+        for turn in ORDER:
+            quarter = lax.rem(home + elems - turn, elems)
+            for source in mates(quarter)[: ring if turn else ring - 1]:
+                flight1(source, pair).wait_recv()
+            if turn == 0:
+                owns[pair].wait()
+            depth = pl.ds(pl.multiple_of(quarter * span, span), span)
+            for first, count in ((0, 512), (512, 512), (1024, 512), (1536, 16)):
+                rows = slice(first, first + count)
+                even = dot(out_table[0, rows, depth], recv1[pair, 0, depth, :])
+                odd = dot(out_table[1, rows, depth], recv1[pair, 1, depth, :])
+                if turn != ORDER[0]:
+                    even = even + phys[0, rows, :]
+                    odd = odd + phys[1, rows, :]
+                if turn != ORDER[-1]:
+                    phys[0, rows, :] = even
+                    phys[1, rows, :] = odd
+                    continue
+                mask = lax.broadcasted_iota(jnp.int32, (count, 128), 1) < 64
+                flux = []
+                for mirror, field in enumerate((even + odd, even - odd)):
+                    if pair:
+                        turned = pltpu.roll(field, 64, 1)
+                        warm[mirror, rows, :] = jnp.where(mask, turned, field) * wet
+                        flux.append(field * turned * wet)
+                    else:
+                        flux.append(field * warm[mirror, rows, :])
+                flux_c[rows, lanes] = (flux[0] + flux[1]).astype(BF16)
+                if count > 16:
+                    flux_s[rows, lanes] = (flux[0] - flux[1]).astype(BF16)
+        mask = lax.broadcasted_iota(jnp.int32, (span, 128), 1) < 64
+        for turn in BACK_ORDER:
+            quarter = lax.rem(home + turn, elems)
+            rows = pl.ds(pl.multiple_of(quarter * span, span), span)
+            even = dot(back_table[0, rows, :], flux_c[:, lanes]) * scale
+            odd = dot(back_table[1, rows, :half], flux_s[:, lanes]) * scale
+            if pair:
+                send2[2, rows, :] = jnp.where(mask, even, odd).astype(BF16)
+            else:
+                send2[0, rows, :] = even.astype(BF16)
+                send2[1, rows, :] = odd.astype(BF16)
+            for dest in mates(quarter)[: ring if turn else ring - 1]:
+                flight2(dest, me, pair).start()
+        planes = pl.ds(2 * pair, 2 - pair)
+        owns[pair] = pltpu.make_async_copy(
+            send2.at[planes, my_rows, :], recv2.at[me, planes], own_sem.at[2 + pair]
+        )
+        owns[pair].start()
+    for k in range(1, parts):
+        for pair in range(2):
+            flight1(lax.rem(me + k, parts), pair).wait_send()
+
+    wave = (lax.broadcasted_iota(jnp.int32, (mode_count, 1), 0) + me * mode_count).astype(F32)
+    wave = wave / modes
+    theta, delta = (4.0, 3.0)
+    powers = jnp.zeros((2 * mode_count, STEPS * 128), F32)
+    for turn in BACK_ORDER:
         quarter = lax.rem(home + elems - turn, elems)
         for source in mates(quarter)[: ring if turn else ring - 1]:
-            flight1(source).wait_recv()
+            for pair in range(2):
+                flight2(source, source, pair).wait_recv()
         if turn == 0:
-            own.wait()
-        depth = pl.ds(pl.multiple_of(quarter * span, span), span)
-        for first, count in ((0, 512), (512, 512), (1024, 512), (1536, 16)):
-            rows = slice(first, first + count)
-            even = dot(out_table[0, rows, depth], recv1[0, depth, :])
-            odd = dot(out_table[1, rows, depth], recv1[1, depth, :])
-            if turn != ORDER[0]:
-                even = even + phys[0, rows, :]
-                odd = odd + phys[1, rows, :]
-            if turn != ORDER[-1]:
-                phys[0, rows, :] = even
-                phys[1, rows, :] = odd
-                continue
-            mask = lax.broadcasted_iota(jnp.int32, (count, 128), 1) < 64
-            flux = []
-            for field in (even + odd, even - odd):
-                last = field[:, 128:]
-                turned = pltpu.roll(last, 64, 1)
-                warm = jnp.where(mask, turned, last) * wet
-                flux.append((field[:, :128] * warm, last * turned * wet))
-            for pair in range(2):
-                lanes = slice(128 * pair, 128 * pair + 128)
-                flux_c[rows, lanes] = (flux[0][pair] + flux[1][pair]).astype(BF16)
-                if count > 16:
-                    flux_s[rows, lanes] = (flux[0][pair] - flux[1][pair]).astype(BF16)
-
-    my_lanes = pl.ds(pl.multiple_of(me * 128, 128), 128)
-
-    def flight2(peer, incoming):
-        rows = pl.ds(pl.multiple_of(peer * mode_count, mode_count), mode_count)
-        return pltpu.make_async_remote_copy(
-            send2.at[:, rows, :],
-            recv2.at[:, :, my_lanes],
-            send2_sem.at[peer],
-            recv2_sem.at[incoming],
-            device_id=(peer, patch),
-            device_id_type=MESH,
-        )
-
-    mask = lax.broadcasted_iota(jnp.int32, (span, 128), 1) < 64
-    for turn in ORDER:
-        quarter = lax.rem(home + turn, elems)
-        rows = pl.ds(pl.multiple_of(quarter * span, span), span)
-        even = dot(back_table[0, rows, :], flux_c[...]) * scale
-        odd = dot(back_table[1, rows, :half], flux_s[...]) * scale
-        send2[0, rows, :] = even[:, :128].astype(BF16)
-        send2[1, rows, :] = odd[:, :128].astype(BF16)
-        send2[2, rows, :] = jnp.where(mask, even[:, 128:], odd[:, 128:]).astype(BF16)
-        for dest in mates(quarter)[: ring if turn else ring - 1]:
-            flight2(dest, me).start()
-    own = pltpu.make_async_copy(send2.at[:, my_rows, :], recv2.at[:, :, my_lanes], own_sem)
-    own.start()
-    for k in range(1, parts):
-        flight1(lax.rem(me + k, parts)).wait_send()
-
-    wave = (lax.broadcasted_iota(jnp.int32, (mode_count, 1), 0) + me * mode_count).astype(F32)
-    wave = wave / modes
-    powers = jnp.zeros((2 * mode_count, STEPS * 128), F32)
-    for turn in ORDER:
-        quarter = lax.rem(home + elems - turn, elems)
-        for source in mates(quarter)[: ring if turn else ring - 1]:
-            flight2(source, source).wait_recv()
-        if turn == 0:
-            own.wait()
-        depth = pl.ds(pl.multiple_of(quarter * 2 * nodes, 2 * nodes), 2 * nodes)
-        moved = dot_nt(
-            recv2[0:2, :, depth].reshape(2 * mode_count, 2 * nodes), weights[quarter]
-        )
+            for own in owns:
+                own.wait()
+        came = [recv2[quarter * ring + k] for k in range(ring)]
+        plane = jnp.concatenate([b[0:2].reshape(2 * mode_count, 128) for b in came], axis=1)
+        moved = dot_nt(plane, weights[quarter])
         around = [[], []]
         for t in range(2):
-            first = quarter * 2 * nodes + 256 * t
-            even = recv2[2, :, pl.ds(pl.multiple_of(first, 128), 128)].astype(F32)
-            odd = recv2[2, :, pl.ds(pl.multiple_of(first + 128, 128), 128)].astype(F32)
-            cosine, sine = split(even, odd)
+            cosine, sine = split(came[2 * t][2].astype(F32), came[2 * t + 1][2].astype(F32))
             around[0].append(-wave * sine)
             around[1].append(wave * cosine)
         around = jnp.concatenate([jnp.concatenate(a, axis=1) for a in around], axis=0)
         lanes = pl.ds(pl.multiple_of(quarter * nodes, nodes), nodes)
         part = heat[:, :, lanes].reshape(2 * mode_count, nodes) - 0.5 * (moved + around)
         forcing[:, lanes] = part
-        powers = powers + dot(part.astype(BF16), pick[lanes, :])
-
-    theta, delta = (4.0, 3.0)
+        part = part.astype(BF16)
+        powers = powers + dot(part, pick[lanes, :])
+        if turn != BACK_ORDER[-1]:
+            told = dot(part, dense[lanes, :])
+            applied[...] = told if turn == BACK_ORDER[0] else applied[...] + told
+
     sigma = theta / delta
     rho = 1.0 / sigma
     keep, take = [], []
@@ -391,14 +411,17 @@
     r1 = p0 - once / theta
     t1 = a0 * t0 + b0 * r1
     t2 = a1 * t1 + b1 * (r1 - ((a0 / theta + b0) * once - (b0 / theta) * twice))
-    traces[0] = t0.astype(BF16)
-    traces[1] = t1.astype(BF16)
-    traces[2] = t2.astype(BF16)
+    part_of = lax.broadcasted_iota(jnp.int32, (2 * mode_count, 128), 1) // (2 * edge)
+    firsts = (t0, pltpu.roll(t1, 2 * edge, 1), pltpu.roll(t2, 4 * edge, 1))
+    lasts = (pltpu.roll(t0, 128 - 2 * edge, 1), t1, pltpu.roll(t2, 2 * edge, 1))
+    for side, (x, y, z) in enumerate((lasts, firsts)):
+        tile = jnp.where(part_of == 0, x, jnp.where(part_of == 1, y, z))
+        traces[side] = tile.astype(BF16)
     flights = []
     for side, dest in enumerate((right, left)):
         flights.append(
             pltpu.make_async_remote_copy(
-                traces,
+                traces.at[side],
                 halo.at[side],
                 halo_send_sem.at[side],
                 halo_recv_sem.at[side],
@@ -414,7 +437,10 @@
     resid = rhs
     walk = resid / theta
     for step in range(STEPS):
-        image = every * walk + dot(walk.astype(BF16), dense[...])
+        if step == 0:
+            image = every * walk + (applied[...] + dot(part, dense[lanes, :])) / theta
+        else:
+            image = every * walk + dot(walk.astype(BF16), dense[...])
         total = total + walk
         resid = resid - image
         walk = keep[step] * walk + take[step] * resid
@@ -425,21 +451,25 @@
     below = lax.broadcasted_iota(jnp.int32, (128, 128), 0) < 2 * edge
     reply0 = jnp.where(below, respond_in[0, 0].astype(F32), respond_in[1, 0].astype(F32)).astype(BF16)
     reply1 = jnp.where(below, respond_in[0, 1].astype(F32), respond_in[1, 1].astype(F32)).astype(BF16)
-    back0 = dot(traces[0], reply0)
-    back1 = dot(traces[1], reply0)
-    back00 = dot(traces[0], reply1)
+    t0, t1 = t0.astype(BF16), t1.astype(BF16)
+    back0 = dot(t0, reply0)
+    back1 = dot(t1, reply0)
+    back00 = dot(t0, reply1)
     around0 = dot(respond[0], reply0).astype(BF16)
 
     for k in range(1, parts):
         peer = lax.rem(me + k, parts)
-        flight2(peer, peer).wait_send()
+        for pair in range(2):
+            flight2(peer, peer, pair).wait_send()
     for flight in flights:
         flight.wait()
-    mine = lax.broadcasted_iota(jnp.int32, (2 * mode_count, 128), 1) < 2 * edge
-    s0, s1, s2 = [
-        jnp.where(mine, halo[1, step].astype(F32), halo[0, step].astype(F32))
-        for step in range(STEPS)
-    ]
+    from_left, from_right = halo[0].astype(F32), halo[1].astype(F32)
+    mine = part_of == 0
+    s0 = jnp.where(mine, from_right, pltpu.roll(from_left, 2 * edge, 1))
+    s1 = jnp.where(mine, pltpu.roll(from_right, 128 - 2 * edge, 1), from_left)
+    s2 = jnp.where(
+        mine, pltpu.roll(from_right, 128 - 4 * edge, 1), pltpu.roll(from_left, 128 - 2 * edge, 1)
+    )
     back1 = back1 + b0 * dot(s0.astype(BF16), around0)
     s1 = s1 + b0 * back0
     first = 1.0 - b0 * wave2
@@ -503,28 +533,30 @@
         scratch_shapes=[pltpu.SMEM(a.shape, a.dtype) for a in small]
         + [pltpu.VMEM(a.shape, a.dtype) for a in big]
         + [
-            pltpu.VMEM((parts, 2, mode_count, 256), BF16),
-            pltpu.VMEM((2, modes, 256), BF16),
-            pltpu.VMEM((2, points // 2 + 16, 256), F32),
+            pltpu.VMEM((parts, 2, 2, mode_count, 128), BF16),
+            pltpu.VMEM((2, 2, modes, 128), BF16),
+            pltpu.VMEM((2, points // 2 + 16, 128), F32),
+            pltpu.VMEM((2, points // 2 + 16, 128), F32),
             pltpu.VMEM((rows, 256), BF16),
             pltpu.VMEM((points // 2, 256), BF16),
             pltpu.VMEM((3, modes, 128), BF16),
-            pltpu.VMEM((3, mode_count, parts * 128), BF16),
+            pltpu.VMEM((parts, 3, mode_count, 128), BF16),
             pltpu.VMEM((elems, nodes, 2 * nodes), BF16),
+            pltpu.VMEM((2 * mode_count, ndev), F32),
             pltpu.VMEM((2 * mode_count, ndev), F32),
             pltpu.VMEM((ndev, ndev), BF16),
             pltpu.VMEM((ndev, STEPS * 128), BF16),
             pltpu.VMEM((STEPS * 128, ndev), BF16),
             pltpu.VMEM((2, 128, 128), BF16),
             pltpu.VMEM((2, 2, 128, 128), BF16),
-            pltpu.VMEM((STEPS, 2 * mode_count, 128), BF16),
-            pltpu.VMEM((2, STEPS, 2 * mode_count, 128), BF16),
+            pltpu.VMEM((2, 2 * mode_count, 128), BF16),
+            pltpu.VMEM((2, 2 * mode_count, 128), BF16),
             pltpu.SemaphoreType.DMA((11,)),
-            pltpu.SemaphoreType.DMA,
-            pltpu.SemaphoreType.DMA((parts,)),
-            pltpu.SemaphoreType.DMA((parts,)),
-            pltpu.SemaphoreType.DMA((parts,)),
-            pltpu.SemaphoreType.DMA((parts,)),
+            pltpu.SemaphoreType.DMA((4,)),
+            pltpu.SemaphoreType.DMA((2, parts)),
+            pltpu.SemaphoreType.DMA((2, parts)),
+            pltpu.SemaphoreType.DMA((2, parts)),
+            pltpu.SemaphoreType.DMA((2, parts)),
             pltpu.SemaphoreType.DMA((2,)),
             pltpu.SemaphoreType.DMA((2,)),
             pltpu.SemaphoreType.DMA((2,)),

time: 47.4 us -> 44.9 us (0.947)
  Pallas kernels: 46.6 us -> 43.9 us
    pallas_call x1, Pallas kernels: 45.8 us -> 43.1 us  [per_device(): pl.pallas_call(functools.partial(kernel, sizes), out_shape=pltpu.VMEM(hea...]
where the time goes in v4:
time: 44.9 us; the launch traced here: 44.8 us
  Pallas kernels  43.9 us (98%)
  between operations  0.82 us (2%)
    pallas_call x1, Pallas kernels, per_device(): pl.pallas_call(functools.partial(kernel, sizes), out_shape=pltpu.VMEM(hea...  43.1 us

profile of v4, /device:TPU:6, one launch (start us, length us, event | category | flops | bytes accessed | tf_op | source)
XLA Modules:
  0.0 44.8 jit_solution(7841034777958637073)
XLA Ops:
  0.7 43.1 %shard_map.118.solved_ref = f32[2,64,1024]{2,1,0:T(8,128)S(1)} custom-call(s32[1,1]{1,0:T(1,128)} %bitcast.1.live_ref, s32[4,4]{1,0:T(4,128)} %partners_hbm.1, s32[4,4]{1,0:T(4,128)} %flags_hbm.1, s32[1,4]{1,0:T(1,128)} %sides_hbm.1, bf16[3,2,64,1024]{3,2,1,0:T(8,128)(2,1)} %flow_hbm.1, f32[2,64,1024]{2,1,0:T(8,128)} %heat_hbm.1, ...), custom_call_target="tpu_custom_call" | custom-call | tf_op jit(solution)/shard_map/pallas_call | solution.py:528
  43.8 0.8 %shard_map.119 = f32[2,64,1024]{2,1,0:T(8,128)} custom-call(f32[2,64,1024]{2,1,0:T(8,128)S(1)} %shard_map.118.solved_ref), custom_call_target="tpu_custom_call" | custom-call | tf_op jit(solution)/shard_map/pallas_call | solution.py:572

commit v5 on v4

--- a/solution.py
+++ b/solution.py
@@ -10,8 +10,7 @@
 from jax.sharding import PartitionSpec as P
 
 STEPS = 3
-ORDER = (2, 1, 3, 0)
-BACK_ORDER = (1, 3, 2, 0)
+ORDER = (1, 3, 2, 0)
 MESH = pl.DeviceIdType.MESH
 F32 = jnp.float32
 BF16 = jnp.bfloat16
@@ -121,7 +120,8 @@
         for i, (src, dst) in enumerate(
             (
                 (heat_hbm, heat),
-                (flow_hbm, flow),
+                (flow_hbm.at[2], flow.at[2]),
+                (flow_hbm.at[pl.ds(0, 2)], flow.at[pl.ds(0, 2)]),
                 (out_table_hbm, out_table),
                 (back_table_hbm, back_table),
                 (slope_hbm, slope),
@@ -134,7 +134,7 @@
             )
         )
     ]
-    for load in loads[:2]:
+    for load in loads[:3]:
         load.start()
 
     barrier = pltpu.get_barrier_semaphore()
@@ -154,7 +154,7 @@
 
     loads[0].wait()
     loads[1].wait()
-    for load in loads[2:]:
+    for load in loads[3:]:
         load.start()
     ring = parts // elems
     home, place = me // ring, lax.rem(me, ring)
@@ -165,7 +165,8 @@
     my_rows = pl.ds(pl.multiple_of(me * mode_count, mode_count), mode_count)
     owns = []
     for pair in (1, 0):
-        lanes = slice(128 * pair, 128 * pair + 128)
+        if not pair:
+            loads[2].wait()
         for turn in ORDER:
             quarter = lax.rem(home + turn, elems)
             for half_tile in range(2):
@@ -197,7 +198,7 @@
         own.start()
         owns.insert(0, own)
 
-    for load in loads[2:]:
+    for load in loads[3:]:
         load.wait()
     lane = lax.broadcasted_iota(jnp.int32, (1, 256), 1)
     group, offset = lane // edge, lane % edge
@@ -342,7 +343,7 @@
                 if count > 16:
                     flux_s[rows, lanes] = (flux[0] - flux[1]).astype(BF16)
         mask = lax.broadcasted_iota(jnp.int32, (span, 128), 1) < 64
-        for turn in BACK_ORDER:
+        for turn in ORDER:
             quarter = lax.rem(home + turn, elems)
             rows = pl.ds(pl.multiple_of(quarter * span, span), span)
             even = dot(back_table[0, rows, :], flux_c[:, lanes]) * scale
@@ -366,32 +367,40 @@
     wave = (lax.broadcasted_iota(jnp.int32, (mode_count, 1), 0) + me * mode_count).astype(F32)
     wave = wave / modes
     theta, delta = (4.0, 3.0)
-    powers = jnp.zeros((2 * mode_count, STEPS * 128), F32)
-    for turn in BACK_ORDER:
+    for turn in ORDER:
         quarter = lax.rem(home + elems - turn, elems)
         for source in mates(quarter)[: ring if turn else ring - 1]:
-            for pair in range(2):
-                flight2(source, source, pair).wait_recv()
+            flight2(source, source, 1).wait_recv()
         if turn == 0:
-            for own in owns:
-                own.wait()
-        came = [recv2[quarter * ring + k] for k in range(ring)]
-        plane = jnp.concatenate([b[0:2].reshape(2 * mode_count, 128) for b in came], axis=1)
-        moved = dot_nt(plane, weights[quarter])
+            owns[1].wait()
         around = [[], []]
         for t in range(2):
-            cosine, sine = split(came[2 * t][2].astype(F32), came[2 * t + 1][2].astype(F32))
+            came = [recv2[quarter * ring + 2 * t + k, 2].astype(F32) for k in range(2)]
+            cosine, sine = split(*came)
             around[0].append(-wave * sine)
             around[1].append(wave * cosine)
         around = jnp.concatenate([jnp.concatenate(a, axis=1) for a in around], axis=0)
         lanes = pl.ds(pl.multiple_of(quarter * nodes, nodes), nodes)
-        part = heat[:, :, lanes].reshape(2 * mode_count, nodes) - 0.5 * (moved + around)
+        forcing[:, lanes] = heat[:, :, lanes].reshape(2 * mode_count, nodes) - 0.5 * around
+    powers = jnp.zeros((2 * mode_count, STEPS * 128), F32)
+    for turn in ORDER:
+        quarter = lax.rem(home + elems - turn, elems)
+        for source in mates(quarter)[: ring if turn else ring - 1]:
+            flight2(source, source, 0).wait_recv()
+        if turn == 0:
+            owns[0].wait()
+        came = [
+            recv2[quarter * ring + k, 0:2].reshape(2 * mode_count, 128) for k in range(ring)
+        ]
+        moved = dot_nt(jnp.concatenate(came, axis=1), weights[quarter])
+        lanes = pl.ds(pl.multiple_of(quarter * nodes, nodes), nodes)
+        part = forcing[:, lanes] - 0.5 * moved
         forcing[:, lanes] = part
         part = part.astype(BF16)
         powers = powers + dot(part, pick[lanes, :])
-        if turn != BACK_ORDER[-1]:
+        if turn != ORDER[-1]:
             told = dot(part, dense[lanes, :])
-            applied[...] = told if turn == BACK_ORDER[0] else applied[...] + told
+            applied[...] = told if turn == ORDER[0] else applied[...] + told
 
     sigma = theta / delta
     rho = 1.0 / sigma
@@ -551,7 +560,7 @@
             pltpu.VMEM((2, 2, 128, 128), BF16),
             pltpu.VMEM((2, 2 * mode_count, 128), BF16),
             pltpu.VMEM((2, 2 * mode_count, 128), BF16),
-            pltpu.SemaphoreType.DMA((11,)),
+            pltpu.SemaphoreType.DMA((12,)),
             pltpu.SemaphoreType.DMA((4,)),
             pltpu.SemaphoreType.DMA((2, parts)),
             pltpu.SemaphoreType.DMA((2, parts)),

time: 44.9 us -> 43 us (0.958)
  Pallas kernels: 43.9 us -> 41.7 us
    pallas_call x1, Pallas kernels: 43.1 us -> 40.9 us  [per_device(): pl.pallas_call(functools.partial(kernel, sizes), out_shape=pltpu.VMEM(hea...]
where the time goes in v5:
time: 43 us; the launch traced here: 42.5 us
  Pallas kernels  41.7 us (97%)
  between operations  0.82 us (2%)
    pallas_call x1, Pallas kernels, per_device(): pl.pallas_call(functools.partial(kernel, sizes), out_shape=pltpu.VMEM(hea...  40.9 us

profile of v5, /device:TPU:6, one launch (start us, length us, event | category | flops | bytes accessed | tf_op | source)
XLA Modules:
  0.0 42.5 jit_solution(16007520560583155110)
XLA Ops:
  0.7 40.9 %shard_map.118.solved_ref = f32[2,64,1024]{2,1,0:T(8,128)S(1)} custom-call(s32[1,1]{1,0:T(1,128)} %bitcast.1.live_ref, s32[4,4]{1,0:T(4,128)} %partners_hbm.1, s32[4,4]{1,0:T(4,128)} %flags_hbm.1, s32[1,4]{1,0:T(1,128)} %sides_hbm.1, bf16[3,2,64,1024]{3,2,1,0:T(8,128)(2,1)} %flow_hbm.1, f32[2,64,1024]{2,1,0:T(8,128)} %heat_hbm.1, ...), custom_call_target="tpu_custom_call" | custom-call | tf_op jit(solution)/shard_map/pallas_call | solution.py:537
  41.6 0.8 %shard_map.119 = f32[2,64,1024]{2,1,0:T(8,128)} custom-call(f32[2,64,1024]{2,1,0:T(8,128)S(1)} %shard_map.118.solved_ref), custom_call_target="tpu_custom_call" | custom-call | tf_op jit(solution)/shard_map/pallas_call | solution.py:581
